TPU v7x, 32 devices: a whole 2x2x4 slice. The times are simulated.
32 devices in a mesh: groups: 2 (over y), along: 4 (over z), cross: 2 (over x), sub: 2 (over core).
Axes of the slice: x: 2, y: 2, z: 4, core: 2. Of those that a mesh axis runs over, the one named last changes fastest.
Arguments:
- state_zero: float32 [12, 64, 512], P(None, ('groups', 'along'), ('cross', 'sub')), parts along dimension 1, may hold values from -6 to 6
- storm_field: float32 [12, 64, 512], P(None, ('groups', 'along'), ('cross', 'sub')), parts along dimension 1, may hold values from -6 to 6
- wet_mask: int32 [2, 64, 512], P(None, ('groups', 'along'), ('cross', 'sub')), parts along dimension 1, may hold values 0 or 1
- dune_mask: int32 [2, 64, 512], P(None, ('groups', 'along'), ('cross', 'sub')), parts along dimension 1, may hold values 0 or 1
- class_ids: int32 [64, 512], P(('groups', 'along'), ('cross', 'sub')), parts along dimension 0, may hold values from 0 to 7
- w_one: float32 [32, 128], replicated, may hold values from -1 to 1
- b_one: float32 [128], replicated, may hold values from -3 to 3
- w_two: float32 [128, 128], replicated, may hold values from -0.5 to 0.5
- b_two: float32 [128], replicated, may hold values from -3 to 3
- w_out: float32 [128, 8], replicated, may hold values from -0.5 to 0.5
- b_out: float32 [8], replicated, may hold values from -3 to 3
- final_cotangent: float32 [12, 64, 512], P(None, ('groups', 'along'), ('cross', 'sub')), parts along dimension 1, may hold values from -6 to 6
Outputs:
- grad_state: float32 [12, 64, 512], P(None, ('groups', 'along'), ('cross', 'sub')), parts along dimension 1
- grad_w_one: float32 [64, 128], P('groups'), parts along dimension 0
- grad_b_one: float32 [256], P('groups'), parts along dimension 0
- grad_w_two: float32 [256, 128], P('groups'), parts along dimension 0
- grad_b_two: float32 [256], P('groups'), parts along dimension 0
- grad_w_out: float32 [256, 8], P('groups'), parts along dimension 0
- grad_b_out: float32 [16], P('groups'), parts along dimension 0
There are 2 independent parts, one for each index of `groups`. A program takes and returns all parts, laid end to end along the dimension named above; an argument that names none is the same for every part. Nothing has to cross between parts.
All inputs are finite; a program needn't handle non-finite values. No bound on the sum of `wet_mask` or of `dune_mask` on one device may be relied on, other than what follows from the above.
Results may differ from a plain program's by a relative error of at most 0.0001.
Values sent between devices are 32-bit elements; how exact they have to be, the bound alone decides.
A program may use at most 64 MiB of HBM per device.

v0:
```python
import math

import jax
import jax.numpy as jnp
from jax import lax
from jax.sharding import PartitionSpec as P

highest = lax.Precision.HIGHEST
diffusion = 0.15
advection = 0.2
friction = 0.05
pickup_gain = 0.5
settling = 0.2
bed_diffusion = 0.1


def with_halo(block, sides, width):
    for axis, dim in sides:
        count = lax.axis_size(axis)
        forward = [(i, i + 1) for i in range(count - 1)]
        backward = [(target, source) for source, target in forward]
        low = lax.ppermute(
            lax.slice_in_dim(block, block.shape[dim] - width, None, axis=dim), axis, forward
        )
        high = lax.ppermute(lax.slice_in_dim(block, 0, width, axis=dim), axis, backward)
        block = jnp.concatenate([low, block, high], axis=dim)
    return block


def layer_stack(weights, features):
    w_one, b_one, w_two, b_two, w_out, b_out = weights
    hidden_one = jax.nn.silu(
        jnp.einsum("fh,frc->hrc", w_one, features, precision=highest) + b_one[:, None, None]
    )
    hidden_two = jax.nn.silu(
        jnp.einsum("hk,hrc->krc", w_two, hidden_one, precision=highest) + b_two[:, None, None]
    )
    return jnp.einsum("ko,krc->orc", w_out, hidden_two, precision=highest) + b_out[:, None, None]


def closure(weights, features):
    return layer_stack(weights, features)


def advance(weights, padded, wet_cells, dune_cells, class_cells, storm_cells):
    centre = padded[:, 1:-1, 1:-1]
    north_cells = padded[:, :-2, 1:-1]
    south_cells = padded[:, 2:, 1:-1]
    west_cells = padded[:, 1:-1, :-2]
    east_cells = padded[:, 1:-1, 2:]
    features = jnp.concatenate(
        [centre[:4], north_cells[:4], south_cells[:4], west_cells[:4], east_cells[:4], storm_cells],
        axis=0,
    )
    outputs = closure(weights, features)
    chooser = (
        class_cells.astype(jnp.float32)[None]
        == jnp.arange(outputs.shape[0], dtype=jnp.float32)[:, None, None]
    ).astype(jnp.float32)
    pickup = jax.nn.softplus(jnp.sum(outputs * chooser, axis=0)) * (1.0 - dune_cells)
    laplace = north_cells + south_cells + west_cells + east_cells - 4.0 * centre
    along_diff = south_cells - north_cells
    cross_diff = east_cells - west_cells
    sediment = centre[4:]
    depth_tend = diffusion * laplace[0] - advection * (along_diff[1] + cross_diff[2])
    along_tend = diffusion * laplace[1] - advection * along_diff[0] - friction * centre[1]
    cross_tend = diffusion * laplace[2] - advection * cross_diff[0] - friction * centre[2]
    bed_tend = (
        bed_diffusion * laplace[3] - pickup_gain * pickup + settling * jnp.sum(sediment, axis=0)
    )
    sediment_tend = (
        diffusion * laplace[4:]
        - advection * (centre[1] * along_diff[4:] + centre[2] * cross_diff[4:])
        + pickup_gain * pickup * chooser
        - settling * sediment
    )
    tendency = jnp.concatenate(
        [jnp.stack([depth_tend, along_tend, cross_tend, bed_tend]), sediment_tend], axis=0
    )
    return centre + wet_cells[None] * tendency


def fold_rims(cot_padded, extended, rim_width):
    double = 2 * rim_width
    interior = cot_padded[:, rim_width:-rim_width, rim_width:-rim_width]
    interior = interior.at[:, :rim_width, :].add(extended[:, :rim_width, double:-double])
    interior = interior.at[:, -rim_width:, :].add(extended[:, -rim_width:, double:-double])
    interior = interior.at[:, :, :rim_width].add(extended[:, double:-double, :rim_width])
    interior = interior.at[:, :, -rim_width:].add(extended[:, double:-double, -rim_width:])
    interior = interior.at[:, :rim_width, :rim_width].add(extended[:, :rim_width, :rim_width])
    interior = interior.at[:, :rim_width, -rim_width:].add(extended[:, :rim_width, -rim_width:])
    interior = interior.at[:, -rim_width:, :rim_width].add(extended[:, -rim_width:, :rim_width])
    interior = interior.at[:, -rim_width:, -rim_width:].add(extended[:, -rim_width:, -rim_width:])
    return interior


def with_edges(field_array):
    return with_halo(field_array, (("along", 1), (("cross", "sub"), 2)), 1)


def return_edges(cot_padded):
    extended = with_halo(cot_padded, (("along", 1), (("cross", "sub"), 2)), 1)
    return fold_rims(cot_padded, extended, 1)


def sum_once(grads):
    return lax.psum(
        (grads[0], grads[1], grads[2], grads[3], grads[4], grads[5]), ("along", "cross", "sub")
    )


def per_device(
    state_zero,
    storm_field,
    wet_mask,
    dune_mask,
    class_ids,
    w_one,
    b_one,
    w_two,
    b_two,
    w_out,
    b_out,
    final_cotangent,
):
    weights = (w_one, b_one, w_two, b_two, w_out, b_out)
    wet_float = wet_mask.astype(jnp.float32)
    dune_float = dune_mask.astype(jnp.float32)
    rows_here = state_zero.shape[1]
    cols_here = state_zero.shape[2]

    def second_step(padded, params):
        return advance(params, padded, wet_float[1], dune_float[1], class_ids, storm_field)

    def first_step(padded, params):
        return advance(params, padded, wet_float[0], dune_float[0], class_ids, storm_field)

    padded_zero = with_edges(state_zero)
    state_one, pull_zero = jax.vjp(first_step, padded_zero, weights)
    padded_one = with_edges(state_one)
    second_state, pull_one = jax.vjp(second_step, padded_one, weights)
    cot_one, grads_one = pull_one(final_cotangent)
    cot_zero, grads_zero = pull_zero(return_edges(cot_one))
    grad_state = return_edges(cot_zero)
    totals = sum_once(jax.tree.map(jnp.add, grads_zero, grads_one))
    factor = 1.0 / math.sqrt(
        rows_here * lax.axis_size("along") * cols_here * lax.axis_size(("cross", "sub"))
    )
    return (
        grad_state,
        totals[0] * factor,
        totals[1] * factor,
        totals[2] * factor,
        totals[3] * factor,
        totals[4] * factor,
        totals[5] * factor,
    )


def solution(mesh):
    return jax.shard_map(
        per_device,
        mesh=mesh,
        in_specs=(
            P(None, ("groups", "along"), ("cross", "sub")),
            P(None, ("groups", "along"), ("cross", "sub")),
            P(None, ("groups", "along"), ("cross", "sub")),
            P(None, ("groups", "along"), ("cross", "sub")),
            P(("groups", "along"), ("cross", "sub")),
            P(),
            P(),
            P(),
            P(),
            P(),
            P(),
            P(None, ("groups", "along"), ("cross", "sub")),
        ),
        out_specs=(
            P(None, ("groups", "along"), ("cross", "sub")),
            P("groups", None),
            P("groups"),
            P("groups", None),
            P("groups"),
            P("groups", None),
            P("groups"),
        ),
        check_vma=False,
    )
```

profile of v0, /device:TPU:0, one launch (start us, length us, event | category | flops | bytes accessed | tf_op | source)
XLA Modules:
  0.0 233.1 jit_solution(9277335089453334680)
XLA Ops:
  8.2 1.4 collective-permute-start.1
  9.6 5.6 %collective-permute-start = (f32[12,1,128]{2,1,0:T(1,128)S(1)}, f32[12,1,128]{2,1,0:T(1,128)S(1)}, u32[]{:S(2)}, u32[]{:S(2)}) collective-permute-start(f32[12,1,128]{2,1,0:T(1,128)S(1)} %get-tuple-element.302), channel_id=1, source_target_pairs={{0,4},{4,8},{8,12},{1,5},{5,9},{9,13},{2,6},{6,10},{10,14},{3,7},{... | collective-permute-start | bytes 18440 | tf_op jit(solution)/shard_map/ppermute | solution.py:22
  17.6 1.3 collective-permute-start.3
  18.9 3.0 %collective-permute-start.2 = (f32[12,10,1]{2,1,0:T(8,128)S(1)}, f32[12,10,1]{2,1,0:T(8,128)S(1)}, u32[]{:S(2)}, u32[]{:S(2)}) collective-permute-start(f32[12,10,1]{2,1,0:T(8,128)S(1)} %get-tuple-element.240), channel_id=1, source_target_pairs={{0,1},{1,2},{2,3},{4,5},{5,6},{6,7},{8,9},{9,10},{10,11},{12,13},{... | collective-permute-start | bytes 1448 | tf_op jit(solution)/shard_map/ppermute | solution.py:22
  24.1 1.0 fusion.1
  26.6 1.3 collective-permute-start.5
  27.9 4.6 %collective-permute-start.4 = (f32[12,1,128]{2,1,0:T(1,128)S(1)}, f32[12,1,128]{2,1,0:T(1,128)S(1)}, u32[]{:S(2)}, u32[]{:S(2)}) collective-permute-start(f32[12,1,128]{2,1,0:T(1,128)S(1)} %get-tuple-element.294), channel_id=1, source_target_pairs={{0,4},{4,8},{8,12},{1,5},{5,9},{9,13},{2,6},{6,10},{10,14},{3,7},{... | collective-permute-start | bytes 18440 | tf_op jit(solution)/shard_map/ppermute | solution.py:22
  32.5 1.3 collective-permute-done.4
  33.9 1.3 collective-permute-start.7
  35.2 3.6 %collective-permute-start.6 = (f32[12,10,1]{2,1,0:T(8,128)S(1)}, f32[12,10,1]{2,1,0:T(8,128)S(1)}, u32[]{:S(2)}, u32[]{:S(2)}) collective-permute-start(f32[12,10,1]{2,1,0:T(8,128)S(1)} %get-tuple-element.238), channel_id=1, source_target_pairs={{0,1},{1,2},{2,3},{4,5},{5,6},{6,7},{8,9},{9,10},{10,11},{12,13},{... | collective-permute-start | bytes 1448 | tf_op jit(solution)/shard_map/ppermute | solution.py:22
  40.2 1.0 fusion
  42.7 1.0 fusion.128
  46.2 1.3 collective-permute-start.9
  47.5 4.5 %collective-permute-start.8 = (f32[12,1,130]{2,1,0:T(1,128)S(1)}, f32[12,1,130]{2,1,0:T(1,128)S(1)}, u32[]{:S(2)}, u32[]{:S(2)}) collective-permute-start(f32[12,1,130]{2,1,0:T(1,128)S(1)} %get-tuple-element.226), channel_id=1, source_target_pairs={{0,4},{4,8},{8,12},{1,5},{5,9},{9,13},{2,6},{6,10},{10,14},{3,7},{... | collective-permute-start | bytes 18728 | tf_op jit(solution)/shard_map/ppermute | solution.py:22
  52.1 1.1 convolution_bitcast_fusion.4
  53.6 1.3 collective-permute-start.11
  54.9 6.5 %collective-permute-start.10 = (f32[12,12,1]{2,1,0:T(8,128)S(1)}, f32[12,12,1]{2,1,0:T(8,128)S(1)}, u32[]{:S(2)}, u32[]{:S(2)}) collective-permute-start(f32[12,12,1]{2,1,0:T(8,128)S(1)} %get-tuple-element.224), channel_id=1, source_target_pairs={{0,1},{1,2},{2,3},{4,5},{5,6},{6,7},{8,9},{9,10},{10,11},{12,13},{... | collective-permute-start | bytes 1736 | tf_op jit(solution)/shard_map/ppermute | solution.py:22
  63.7 1.9 broadcast_select_fusion.1
  65.6 2.1 scatter-add.61
  68.0 1.1 scatter-add.65
  70.0 1.0 fusion.127
  73.2 1.7 fusion.4
  75.4 64.9 %all-reduce.50 = (f32[32,128]{1,0:T(8,128)S(1)}, f32[128]{0:T(128)S(1)}, f32[128]{0:T(128)S(1)}, f32[128,8]{0,1:T(8,128)S(1)}, f32[8]{0:T(128)S(1)}) all-reduce(f32[32,128]{1,0:T(8,128)S(1)} %fusion.5, f32[128]{0:T(128)S(1)} %add.408, ...), channel_id=1, replica_groups=mesh['groups'=2,'along'=4,'cross'=2,'sub'=2] {'along','cross','sub'}, use_global_device_ids=true, to_apply=%region_10.11 | all-reduce | flops 5384 | bytes 43072 | tf_op jit(solution)/shard_map/psum | solution.py:107
  142.0 1.3 collective-permute-start.13
  143.3 4.5 %collective-permute-start.12 = (f32[12,1,130]{2,1,0:T(1,128)S(1)}, f32[12,1,130]{2,1,0:T(1,128)S(1)}, u32[]{:S(2)}, u32[]{:S(2)}) collective-permute-start(f32[12,1,130]{2,1,0:T(1,128)S(1)} %get-tuple-element.222), channel_id=1, source_target_pairs={{0,4},{4,8},{8,12},{1,5},{5,9},{9,13},{2,6},{6,10},{10,14},{3,7},{... | collective-permute-start | bytes 18728 | tf_op jit(solution)/shard_map/ppermute | solution.py:22
  149.4 1.3 collective-permute-start.14
  151.0 1.3 collective-permute-start.15
  152.4 1.7 collective-permute-done.15
  155.3 1.9 broadcast_select_fusion
  157.3 2.1 scatter-add.75
  160.6 64.1 %all-reduce.53.cloned.1.call-done = f32[128,128]{1,0:T(8,128)} async-done(((f32[128,128]{1,0:T(8,128)}), f32[128,128]{1,0:T(8,128)}) %all-reduce.53.cloned.1.call-update) | async-done | bytes 65552 | tf_op jit(solution)/shard_map/psum | solution.py:107
  224.7 1.5 broadcast_multiply_fusion
  (165 shorter events, 24.2 us)
Async XLA Ops:
  7.2 17.9 %copy-start = (f32[128,128]{1,0:T(8,128)S(1)}, f32[128,128]{1,0:T(8,128)}, u32[]{:S(2)}) copy-start(f32[128,128]{1,0:T(8,128)} %param.51) | copy-start | bytes 196612
  7.2 8.8 %copy-start.1 = (f32[12,8,128]{2,1,0:T(8,128)S(1)}, f32[12,8,128]{2,1,0:T(8,128)}, u32[]{:S(2)}) copy-start(f32[12,8,128]{2,1,0:T(8,128)} %param.44) | copy-start | bytes 147460
  7.2 217.5 %all-reduce.53.cloned.1.call-start = ((), (), s32[]{:S(2)}) async-start(), calls=%async_computation | async-start | bytes 131072 | tf_op jit(solution)/shard_map/psum | solution.py:107
  7.2 8.7 %copy-start.6 = (s32[2,8,128]{2,1,0:T(8,128)S(1)}, s32[2,8,128]{2,1,0:T(8,128)}, u32[]{:S(2)}) copy-start(s32[2,8,128]{2,1,0:T(8,128)} %param.46) | copy-start | bytes 24580
  8.1 7.9 %copy-start.4 = (f32[12,8,128]{2,1,0:T(8,128)S(1)}, f32[12,8,128]{2,1,0:T(8,128)}, u32[]{:S(2)}) copy-start(f32[12,8,128]{2,1,0:T(8,128)} %param.55) | copy-start | bytes 147460
  8.2 9.2 %collective-permute-start.1 = (f32[12,1,128]{2,1,0:T(1,128)S(1)}, f32[12,1,128]{2,1,0:T(1,128)S(1)}, u32[]{:S(2)}, u32[]{:S(2)}) collective-permute-start(f32[12,1,128]{2,1,0:T(1,128)S(1)} %get-tuple-element.301), channel_id=1, source_target_pairs={{4,0},{8,4},{12,8},{5,1},{9,5},{13,9},{6,2},{10,6},{14,10},{7,3},{... | collective-permute-start | bytes 18440 | tf_op jit(solution)/shard_map/ppermute | solution.py:25
  9.6 7.8 %collective-permute-start = (f32[12,1,128]{2,1,0:T(1,128)S(1)}, f32[12,1,128]{2,1,0:T(1,128)S(1)}, u32[]{:S(2)}, u32[]{:S(2)}) collective-permute-start(f32[12,1,128]{2,1,0:T(1,128)S(1)} %get-tuple-element.302), channel_id=1, source_target_pairs={{0,4},{4,8},{8,12},{1,5},{5,9},{9,13},{2,6},{6,10},{10,14},{3,7},{... | collective-permute-start | bytes 18440 | tf_op jit(solution)/shard_map/ppermute | solution.py:22
  16.0 0.7 copy-start.12
  17.4 5.1 %copy-start.8 = (s32[8,128]{1,0:T(8,128)S(1)}, s32[8,128]{1,0:T(8,128)}, u32[]{:S(2)}) copy-start(s32[8,128]{1,0:T(8,128)} %param.48) | copy-start | bytes 12292
  17.4 5.1 %copy-start.5 = (f32[12,8,128]{2,1,0:T(8,128)S(1)}, f32[12,8,128]{2,1,0:T(8,128)}, u32[]{:S(2)}) copy-start(f32[12,8,128]{2,1,0:T(8,128)} %param.45) | copy-start | bytes 147460
  17.5 4.9 %copy-start.7 = (s32[2,8,128]{2,1,0:T(8,128)S(1)}, s32[2,8,128]{2,1,0:T(8,128)}, u32[]{:S(2)}) copy-start(s32[2,8,128]{2,1,0:T(8,128)} %param.47) | copy-start | bytes 24580
  17.6 5.0 %collective-permute-start.3 = (f32[12,10,1]{2,1,0:T(8,128)S(1)}, f32[12,10,1]{2,1,0:T(8,128)S(1)}, u32[]{:S(2)}, u32[]{:S(2)}) collective-permute-start(f32[12,10,1]{2,1,0:T(8,128)S(1)} %get-tuple-element.239), channel_id=1, source_target_pairs={{1,0},{2,1},{3,2},{5,4},{6,5},{7,6},{9,8},{10,9},{11,10},{13,12},{... | collective-permute-start | bytes 1448 | tf_op jit(solution)/shard_map/ppermute | solution.py:25
  18.9 4.0 %collective-permute-start.2 = (f32[12,10,1]{2,1,0:T(8,128)S(1)}, f32[12,10,1]{2,1,0:T(8,128)S(1)}, u32[]{:S(2)}, u32[]{:S(2)}) collective-permute-start(f32[12,10,1]{2,1,0:T(8,128)S(1)} %get-tuple-element.240), channel_id=1, source_target_pairs={{0,1},{1,2},{2,3},{4,5},{5,6},{6,7},{8,9},{9,10},{10,11},{12,13},{... | collective-permute-start | bytes 1448 | tf_op jit(solution)/shard_map/ppermute | solution.py:22
  23.4 0.7 copy-start.3
  23.4 0.7 copy-start.9
  24.1 1.0 copy-start.14
  25.1 0.7 copy-start.13
  25.8 0.7 copy-start.11
  26.6 5.9 %collective-permute-start.5 = (f32[12,1,128]{2,1,0:T(1,128)S(1)}, f32[12,1,128]{2,1,0:T(1,128)S(1)}, u32[]{:S(2)}, u32[]{:S(2)}) collective-permute-start(f32[12,1,128]{2,1,0:T(1,128)S(1)} %get-tuple-element.293), channel_id=1, source_target_pairs={{4,0},{8,4},{12,8},{5,1},{9,5},{13,9},{6,2},{10,6},{14,10},{7,3},{... | collective-permute-start | bytes 18440 | tf_op jit(solution)/shard_map/ppermute | solution.py:25
  27.9 5.9 %collective-permute-start.4 = (f32[12,1,128]{2,1,0:T(1,128)S(1)}, f32[12,1,128]{2,1,0:T(1,128)S(1)}, u32[]{:S(2)}, u32[]{:S(2)}) collective-permute-start(f32[12,1,128]{2,1,0:T(1,128)S(1)} %get-tuple-element.294), channel_id=1, source_target_pairs={{0,4},{4,8},{8,12},{1,5},{5,9},{9,13},{2,6},{6,10},{10,14},{3,7},{... | collective-permute-start | bytes 18440 | tf_op jit(solution)/shard_map/ppermute | solution.py:22
  33.9 5.0 %collective-permute-start.7 = (f32[12,10,1]{2,1,0:T(8,128)S(1)}, f32[12,10,1]{2,1,0:T(8,128)S(1)}, u32[]{:S(2)}, u32[]{:S(2)}) collective-permute-start(f32[12,10,1]{2,1,0:T(8,128)S(1)} %get-tuple-element.237), channel_id=1, source_target_pairs={{1,0},{2,1},{3,2},{5,4},{6,5},{7,6},{9,8},{10,9},{11,10},{13,12},{... | collective-permute-start | bytes 1448 | tf_op jit(solution)/shard_map/ppermute | solution.py:25
  35.2 4.6 %collective-permute-start.6 = (f32[12,10,1]{2,1,0:T(8,128)S(1)}, f32[12,10,1]{2,1,0:T(8,128)S(1)}, u32[]{:S(2)}, u32[]{:S(2)}) collective-permute-start(f32[12,10,1]{2,1,0:T(8,128)S(1)} %get-tuple-element.238), channel_id=1, source_target_pairs={{0,1},{1,2},{2,3},{4,5},{5,6},{6,7},{8,9},{9,10},{10,11},{12,13},{... | collective-permute-start | bytes 1448 | tf_op jit(solution)/shard_map/ppermute | solution.py:22
  45.2 0.7 copy-start.10
  46.2 7.0 %collective-permute-start.9 = (f32[12,1,130]{2,1,0:T(1,128)S(1)}, f32[12,1,130]{2,1,0:T(1,128)S(1)}, u32[]{:S(2)}, u32[]{:S(2)}) collective-permute-start(f32[12,1,130]{2,1,0:T(1,128)S(1)} %get-tuple-element.225), channel_id=1, source_target_pairs={{4,0},{8,4},{12,8},{5,1},{9,5},{13,9},{6,2},{10,6},{14,10},{7,3},{... | collective-permute-start | bytes 18728 | tf_op jit(solution)/shard_map/ppermute | solution.py:25
  47.5 5.9 %collective-permute-start.8 = (f32[12,1,130]{2,1,0:T(1,128)S(1)}, f32[12,1,130]{2,1,0:T(1,128)S(1)}, u32[]{:S(2)}, u32[]{:S(2)}) collective-permute-start(f32[12,1,130]{2,1,0:T(1,128)S(1)} %get-tuple-element.226), channel_id=1, source_target_pairs={{0,4},{4,8},{8,12},{1,5},{5,9},{9,13},{2,6},{6,10},{10,14},{3,7},{... | collective-permute-start | bytes 18728 | tf_op jit(solution)/shard_map/ppermute | solution.py:22
  53.6 8.9 %collective-permute-start.11 = (f32[12,12,1]{2,1,0:T(8,128)S(1)}, f32[12,12,1]{2,1,0:T(8,128)S(1)}, u32[]{:S(2)}, u32[]{:S(2)}) collective-permute-start(f32[12,12,1]{2,1,0:T(8,128)S(1)} %get-tuple-element.223), channel_id=1, source_target_pairs={{1,0},{2,1},{3,2},{5,4},{6,5},{7,6},{9,8},{10,9},{11,10},{13,12},{... | collective-permute-start | bytes 1736 | tf_op jit(solution)/shard_map/ppermute | solution.py:25
  54.9 7.5 %collective-permute-start.10 = (f32[12,12,1]{2,1,0:T(8,128)S(1)}, f32[12,12,1]{2,1,0:T(8,128)S(1)}, u32[]{:S(2)}, u32[]{:S(2)}) collective-permute-start(f32[12,12,1]{2,1,0:T(8,128)S(1)} %get-tuple-element.224), channel_id=1, source_target_pairs={{0,1},{1,2},{2,3},{4,5},{5,6},{6,7},{8,9},{9,10},{10,11},{12,13},{... | collective-permute-start | bytes 1736 | tf_op jit(solution)/shard_map/ppermute | solution.py:22
  142.0 7.0 %collective-permute-start.13 = (f32[12,1,130]{2,1,0:T(1,128)S(1)}, f32[12,1,130]{2,1,0:T(1,128)S(1)}, u32[]{:S(2)}, u32[]{:S(2)}) collective-permute-start(f32[12,1,130]{2,1,0:T(1,128)S(1)} %get-tuple-element.221), channel_id=1, source_target_pairs={{4,0},{8,4},{12,8},{5,1},{9,5},{13,9},{6,2},{10,6},{14,10},{7,3},{... | collective-permute-start | bytes 18728 | tf_op jit(solution)/shard_map/ppermute | solution.py:25
  143.3 5.9 %collective-permute-start.12 = (f32[12,1,130]{2,1,0:T(1,128)S(1)}, f32[12,1,130]{2,1,0:T(1,128)S(1)}, u32[]{:S(2)}, u32[]{:S(2)}) collective-permute-start(f32[12,1,130]{2,1,0:T(1,128)S(1)} %get-tuple-element.222), channel_id=1, source_target_pairs={{0,4},{4,8},{8,12},{1,5},{5,9},{9,13},{2,6},{6,10},{10,14},{3,7},{... | collective-permute-start | bytes 18728 | tf_op jit(solution)/shard_map/ppermute | solution.py:22
  149.4 2.9 %collective-permute-start.14 = (f32[12,12,1]{2,1,0:T(8,128)S(1)}, f32[12,12,1]{2,1,0:T(8,128)S(1)}, u32[]{:S(2)}, u32[]{:S(2)}) collective-permute-start(f32[12,12,1]{2,1,0:T(8,128)S(1)} %get-tuple-element.220), channel_id=1, source_target_pairs={{0,1},{1,2},{2,3},{4,5},{5,6},{6,7},{8,9},{9,10},{10,11},{12,13},{... | collective-permute-start | bytes 1736 | tf_op jit(solution)/shard_map/ppermute | solution.py:22
  151.0 3.2 %collective-permute-start.15 = (f32[12,12,1]{2,1,0:T(8,128)S(1)}, f32[12,12,1]{2,1,0:T(8,128)S(1)}, u32[]{:S(2)}, u32[]{:S(2)}) collective-permute-start(f32[12,12,1]{2,1,0:T(8,128)S(1)} %get-tuple-element.219), channel_id=1, source_target_pairs={{1,0},{2,1},{3,2},{5,4},{6,5},{7,6},{9,8},{10,9},{11,10},{13,12},{... | collective-permute-start | bytes 1736 | tf_op jit(solution)/shard_map/ppermute | solution.py:25
  160.6 65.6 %copy-start.2 = (f32[12,8,128]{2,1,0:T(8,128)}, f32[12,8,128]{2,1,0:T(8,128)S(1)}, u32[]{:S(2)}) copy-start(f32[12,8,128]{2,1,0:T(8,128)S(1)} %scatter-add.79) | copy-start | bytes 147460
Sparse Core Ops, SparseCore 0:
  141.0 83.6 all-reduce.52
where the time goes:
time: 235 us; the launch traced here: 233 us
  waiting for transfers between devices  69.5 us (30%)
  blocking collectives  64.9 us (28%)
  starting transfers between devices  44.2 us (19%)
  between operations  15 us (6%)
  matrix products  13.8 us (6%)
  local copies, waits for them, and re-layouts  13.7 us (6%)
  other arithmetic  11.8 us (5%)
    psum x1, blocking collectives, sum_once(): lax.psum((grads[0], grads[1], grads[2], grads[3], grads[4], grads[5]), ('...  64.9 us
    psum x1, waiting for transfers between devices, sum_once(): lax.psum((grads[0], grads[1], grads[2], grads[3], grads[4], grads[5]), ('...  64.1 us
    ppermute x8, starting transfers between devices, with_halo(): lax.ppermute(lax.slice_in_dim(block, block.shape[dim] - width, None, axis...  33.7 us
    ppermute x8, starting transfers between devices, with_halo(): lax.ppermute(lax.slice_in_dim(block, 0, width, axis=dim), axis, backward)  10.5 us
    dot_general x6, matrix products, layer_stack(): jnp.einsum('hk,hrc->krc', w_two, hidden_one, precision=highest)  5.42 us
  transfers between devices with their start and end apart: 17, of which 8 were waited for; matrix products, arithmetic and copies ran while one was open for 5% of the time, Pallas kernels for 0%

commit v1 on v0

v1 whole, which is shorter than its diff:
```python
import functools
import math

import jax
import jax.numpy as jnp
from jax import lax
from jax.experimental import pallas as pl
from jax.experimental.pallas import tpu as pltpu
from jax.sharding import PartitionSpec as P

MESH = pl.DeviceIdType.MESH
f32 = jnp.float32
bf16 = jnp.bfloat16
diffusion = 0.15
advection = 0.2
friction = 0.05
pickup_gain = 0.5
settling = 0.2
bed_diffusion = 0.1

ROW_B1 = 32
ROW_W2 = 40
ROW_B2 = 168
ROW_WO = 176
ROW_BO = 184
PACK_ROWS = 192
LANES = 256
CHUNKS = 4


def split(x):
    high = x.astype(bf16)
    low = (x - high.astype(f32)).astype(bf16)
    return high, low


def mm(a, b):
    return lax.dot_general(a, b, (((1,), (0,)), ((), ())), preferred_element_type=f32)


def mm_nt(a, b):
    return lax.dot_general(a, b, (((1,), (1,)), ((), ())), preferred_element_type=f32)


def kernel(
    nal, ncr, nsu, chunk_rows, factor,
    state_ref, storm_ref, wet_ref, dune_ref, cid_ref,
    w1_ref, b1_ref, w2_ref, b2_ref, wo_ref, bo_ref, cot_ref,
    gstate_ref, gw1_ref, gb1_ref, gw2_ref, gb2_ref, gwo_ref, gbo_ref,
    snd_row, snd_col, rcv_row, rcv_col, send_sem, recv_sem,
    feat_ref, dfeat_ref, z_ref, dz_ref,
    b1b_ref, b2b_ref, wsel_ref,
    fh_ref, fl_ref, h1h_ref, h1l_ref, h2h_ref, h2l_ref,
    act1_ref, q2_ref, d1h_ref, d1l_ref, d2h_ref, d2l_ref, drh_ref, drl_ref,
    acc_ref, rcv_a, src_b, rcv_b, full_ref,
    sa_send, sa_recv, sb_send, sb_recv, sc_send, sc_recv,
):
    ncs = ncr * nsu
    g = lax.axis_index("groups")
    al = lax.axis_index("along")
    cr = lax.axis_index("cross")
    su = lax.axis_index("sub")
    cs = cr * nsu + su

    def dev(a, c):
        return (g, a, c // nsu, c % nsu)

    has_dst = (al > 0, al < nal - 1, cs > 0, cs < ncs - 1)
    has_src = (al < nal - 1, al > 0, cs < ncs - 1, cs > 0)
    dst_dev = (
        dev(al - 1, cs), dev(al + 1, cs), dev(al, cs - 1), dev(al, cs + 1),
    )

    rcv_row[...] = jnp.zeros_like(rcv_row)
    rcv_col[...] = jnp.zeros_like(rcv_col)

    barrier = pltpu.get_barrier_semaphore()
    for j in range(1, ncs):
        pl.semaphore_signal(
            barrier, inc=1, device_id=dev(al, lax.rem(cs + j, ncs)), device_id_type=MESH
        )
    for j in range(1, nal):
        pl.semaphore_signal(
            barrier, inc=1, device_id=dev(lax.rem(al + j, nal), cs), device_id_type=MESH
        )

    row = lax.broadcasted_iota(jnp.int32, (8, 128), 0)
    lane = lax.broadcasted_iota(jnp.int32, (8, 128), 1)

    def copy_of(k, d):
        if d < 2:
            src, dst = snd_row.at[k, d], rcv_row.at[k, d]
        else:
            src, dst = snd_col.at[k, d - 2], rcv_col.at[k, d - 2]
        return pltpu.make_async_remote_copy(
            src_ref=src, dst_ref=dst, send_sem=send_sem.at[k, d], recv_sem=recv_sem.at[k, d],
            device_id=dst_dev[d], device_id_type=MESH,
        )

    def fill(k, xn, xs, xw, xe):
        west = jnp.zeros((8, 128), f32)
        east = jnp.zeros((8, 128), f32)
        for f in range(12):
            snd_row[k, 0, f:f + 1, :] = xn[f][0:1, :]
            snd_row[k, 1, f:f + 1, :] = xs[f][7:8, :]
            west = jnp.where(lane == f, pltpu.roll(xw[f], f, 1) if f else xw[f], west)
            east = jnp.where(lane == f, pltpu.roll(xe[f], f + 1, 1), east)
        snd_col[k, 0] = west
        snd_col[k, 1] = east

    def launch(k):
        for d in range(4):
            @pl.when(has_dst[d])
            def _():
                copy_of(k, d).start()

    def finish(k):
        for d in range(4):
            @pl.when(has_src[d])
            def _():
                copy_of(k, d).wait_recv()

    def finish_sends(k):
        for d in range(4):
            @pl.when(has_dst[d])
            def _():
                copy_of(k, d).wait_send()

    def south_of(x, f, k):
        return jnp.where(row == 7, rcv_row[k, 0, f:f + 1, :], pltpu.roll(x, 7, 0))

    def north_of(x, f, k):
        return jnp.where(row == 0, rcv_row[k, 1, f:f + 1, :], pltpu.roll(x, 1, 0))

    def east_of(x, f, k):
        return jnp.where(lane == 127, pltpu.roll(rcv_col[k, 0], 127 - f, 1), pltpu.roll(x, 127, 1))

    def west_of(x, f, k):
        halo = rcv_col[k, 1]
        return jnp.where(lane == 0, pltpu.roll(halo, 128 - f, 1) if f else halo, pltpu.roll(x, 1, 1))

    V0 = [state_ref[f] for f in range(12)]
    fill(0, V0, V0, V0, V0)
    pl.semaphore_wait(barrier, ncs - 1 + nal - 1)
    launch(0)

    w1 = w1_ref[...]
    w1t = jnp.transpose(jnp.concatenate([w1, jnp.zeros((96, 128), f32)], axis=0))[:, :32]
    w1th, w1tl = split(w1t)
    w1t_cat = jnp.concatenate([w1th, w1tl, w1th], axis=1)
    w1h, w1l = split(w1)
    w1_hh = jnp.concatenate([w1h, w1h], axis=1)
    w2 = w2_ref[...]
    w2h, w2l = split(w2)
    w2_hh = jnp.concatenate([w2h, w2h], axis=1)
    w2th, w2tl = split(jnp.transpose(w2))
    w2t_hh = jnp.concatenate([w2th, w2th], axis=1)
    b1b_ref[...] = jnp.transpose(jnp.broadcast_to(b1_ref[...], (128, 128)))
    b2b_ref[...] = jnp.transpose(jnp.broadcast_to(b2_ref[...], (128, 128)))
    cid = cid_ref[...]
    wo = wo_ref[...]
    for r in range(8):
        onehot = (lax.broadcasted_iota(jnp.int32, (8, 128), 0) == cid[r:r + 1, :]).astype(f32)
        wsel_ref[:, r * 128:(r + 1) * 128] = lax.dot_general(
            wo, onehot, (((1,), (0,)), ((), ())),
            precision=lax.Precision.HIGHEST, preferred_element_type=f32,
        )
    bsel = jnp.zeros((8, 128), f32)
    for k in range(8):
        bsel = jnp.where(cid == k, bo_ref[k], bsel)
    for f in range(12):
        feat_ref[(20 + f) * 8:(21 + f) * 8, :] = storm_ref[f]
    wets = [wet_ref[t].astype(f32) for t in range(2)]
    wash = [1.0 - dune_ref[t].astype(f32) for t in range(2)]

    def forward(t, V, k):
        near = []
        for f in range(12):
            n, s = north_of(V[f], f, k), south_of(V[f], f, k)
            w, e = west_of(V[f], f, k), east_of(V[f], f, k)
            near.append((n, s, w, e))
            if f < 4:
                feat_ref[f * 8:(f + 1) * 8, :] = V[f]
                feat_ref[(4 + f) * 8:(5 + f) * 8, :] = n
                feat_ref[(8 + f) * 8:(9 + f) * 8, :] = s
                feat_ref[(12 + f) * 8:(13 + f) * 8, :] = w
                feat_ref[(16 + f) * 8:(17 + f) * 8, :] = e
        for c in range(CHUNKS):
            at = pl.ds(c * LANES, LANES)
            F = jnp.concatenate(
                [feat_ref[pl.ds(2 * c + i, 32, stride=8), :] for i in range(2)], axis=1
            )
            Fh, Fl = split(F)
            fh_ref[t, :, at] = Fh
            fl_ref[t, :, at] = Fl
            v = mm(w1t_cat, jnp.concatenate([Fh, Fh, Fl], axis=0))
            bias = b1b_ref[...]
            v = v + jnp.concatenate([bias, bias], axis=1)
            sig = 1.0 / (1.0 + jnp.exp(-v))
            h = v * sig
            act1_ref[t, :, at] = sig + h * (1.0 - sig)
            Hh, Hl = split(h)
            h1h_ref[t, :, at] = Hh
            h1l_ref[t, :, at] = Hl
            v = mm(w2t_hh, jnp.concatenate([Hh, Hl], axis=0)) + mm(w2tl, Hh)
            bias = b2b_ref[...]
            v = v + jnp.concatenate([bias, bias], axis=1)
            sig = 1.0 / (1.0 + jnp.exp(-v))
            h = v * sig
            wsel = wsel_ref[:, at]
            q2_ref[t, :, at] = wsel * (sig + h * (1.0 - sig))
            z = jnp.sum(wsel * h, axis=0, keepdims=True)
            Hh, Hl = split(h)
            h2h_ref[t, :, at] = Hh
            h2l_ref[t, :, at] = Hl
            for i in range(2):
                z_ref[2 * c + i:2 * c + i + 1, :] = z[:, i * 128:(i + 1) * 128]
        return near, z_ref[...] + bsel

    def backward(t, z, near, V, lam):
        G = [wets[t] * lam[f] for f in range(12)]
        picked = G[4]
        for k in range(1, 8):
            picked = jnp.where(cid == k, G[4 + k], picked)
        gate = 1.0 / (1.0 + jnp.exp(-z))
        dz = pickup_gain * (picked - G[3]) * wash[t] * gate
        dz_ref[...] = dz
        for c in range(CHUNKS):
            at = pl.ds(c * LANES, LANES)
            drow = jnp.concatenate(
                [dz_ref[2 * c + i:2 * c + i + 1, :] for i in range(2)], axis=1
            )
            d2 = q2_ref[t, :, at] * drow
            Dh, Dl = split(d2)
            d2h_ref[t, :, at] = Dh
            d2l_ref[t, :, at] = Dl
            d1 = mm(w2_hh, jnp.concatenate([Dh, Dl], axis=0)) + mm(w2l, Dh)
            d1 = d1 * act1_ref[t, :, at]
            Dh, Dl = split(d1)
            d1h_ref[t, :, at] = Dh
            d1l_ref[t, :, at] = Dl
            dF = mm(w1_hh, jnp.concatenate([Dh, Dl], axis=0)) + mm(w1l, Dh)
            for i in range(2):
                dfeat_ref[pl.ds(2 * c + i, 32, stride=8), :] = dF[:, i * 128:(i + 1) * 128]
        D = [dfeat_ref[f * 8:(f + 1) * 8, :] for f in range(20)]
        lap = [bed_diffusion if f == 3 else diffusion for f in range(12)]
        lg = [lap[f] * G[f] for f in range(12)]
        c = [lam[f] - 4.0 * lg[f] for f in range(12)]
        alongs = jnp.zeros((8, 128), f32)
        crosses = jnp.zeros((8, 128), f32)
        along_part = [advection * G[1], advection * G[0], None, None]
        cross_part = [advection * G[2], None, advection * G[0], None]
        for k in range(8):
            n, s, w, e = near[4 + k]
            alongs = alongs + (s - n) * G[4 + k]
            crosses = crosses + (e - w) * G[4 + k]
            c[4 + k] = c[4 + k] + settling * (G[3] - G[4 + k])
            ag = advection * G[4 + k]
            along_part.append(V[1] * ag)
            cross_part.append(V[2] * ag)
        c[1] = c[1] - friction * G[1] - advection * alongs
        c[2] = c[2] - friction * G[2] - advection * crosses
        to = [[], [], [], []]
        for f in range(12):
            for d, part, sign in ((0, along_part, 1), (1, along_part, -1), (2, cross_part, 1), (3, cross_part, -1)):
                x = lg[f]
                if part[f] is not None:
                    x = x + part[f] if sign > 0 else x - part[f]
                if f < 4:
                    x = x + D[4 + 4 * d + f]
                to[d].append(x)
            if f < 4:
                c[f] = c[f] + D[f]
        return dz, c, to

    def gather(c, to, k):
        return [
            c[f] + south_of(to[0][f], f, k) + north_of(to[1][f], f, k)
            + east_of(to[2][f], f, k) + west_of(to[3][f], f, k)
            for f in range(12)
        ]

    def weight_grads(t, dz, first):
        ones = jnp.ones((16, 1024), bf16)
        chooser_rows = []
        for r in range(8):
            onehot = lax.broadcasted_iota(jnp.int32, (8, 128), 0) == cid[r:r + 1, :]
            chooser_rows.append(jnp.where(onehot, dz[r:r + 1, :], 0.0))
        dr = jnp.concatenate(chooser_rows, axis=1)
        dbo = jnp.broadcast_to(jnp.sum(dr, axis=1, keepdims=True), (8, 128))
        pad = jnp.zeros((8, 1024), f32)
        drh, drl = split(jnp.concatenate([dr, pad], axis=0))
        h2h, h2l = h2h_ref[t], h2l_ref[t]
        top = mm_nt(jnp.concatenate([drh, drl], axis=0), h2h)
        dwo = top[:8] + top[16:24] + mm_nt(drh, h2l)[:8]
        lhs = jnp.concatenate([h1h_ref[t], ones, h1l_ref[t]], axis=0)
        top = mm_nt(lhs, d2h_ref[t])
        low = mm_nt(lhs[:144], d2l_ref[t])
        dw2 = top[:128] + top[144:272] + low[:128]
        db2 = top[128:136] + low[128:136]
        lhs = jnp.concatenate([fh_ref[t], ones, fl_ref[t]], axis=0)
        top = mm_nt(lhs, d1h_ref[t])
        low = mm_nt(lhs[:48], d1l_ref[t])
        dw1 = top[:32] + top[48:80] + low[:32]
        db1 = top[32:40] + low[32:40]
        for start, part in ((0, dw1), (ROW_B1, db1), (ROW_W2, dw2), (ROW_B2, db2), (ROW_WO, dwo), (ROW_BO, dbo)):
            at = pl.ds(start, part.shape[0])
            acc_ref[at, :] = part if first else acc_ref[at, :] + part

    finish(0)
    near0, z0 = forward(0, V0, 0)
    soft = jnp.maximum(z0, 0.0) + jnp.log(1.0 + jnp.exp(-jnp.abs(z0)))
    pickup = soft * wash[0]
    V1 = []
    lap = []
    for f in range(12):
        n, s, w, e = near0[f]
        lap.append(n + s + w + e - 4.0 * V0[f])
    total = V0[4]
    for k in range(1, 8):
        total = total + V0[4 + k]
    ad = [near0[f][1] - near0[f][0] for f in range(12)]
    cd = [near0[f][3] - near0[f][2] for f in range(12)]
    tend = [
        diffusion * lap[0] - advection * (ad[1] + cd[2]),
        diffusion * lap[1] - advection * ad[0] - friction * V0[1],
        diffusion * lap[2] - advection * cd[0] - friction * V0[2],
        bed_diffusion * lap[3] - pickup_gain * pickup + settling * total,
    ]
    for k in range(8):
        x = diffusion * lap[4 + k] - advection * (V0[1] * ad[4 + k] + V0[2] * cd[4 + k])
        x = x + jnp.where(cid == k, pickup_gain * pickup, 0.0) - settling * V0[4 + k]
        tend.append(x)
    V1 = [V0[f] + wets[0] * tend[f] for f in range(12)]
    fill(1, V1, V1, V1, V1)
    launch(1)
    finish(1)

    near1, z1 = forward(1, V1, 1)
    lam2 = [cot_ref[f] for f in range(12)]
    dz1, c1, to1 = backward(1, z1, near1, V1, lam2)
    fill(2, *to1)
    launch(2)
    weight_grads(1, dz1, True)
    finish(2)
    lam1 = gather(c1, to1, 2)

    dz0, c0, to0 = backward(0, z0, near0, V0, lam1)
    fill(3, *to0)
    launch(3)
    weight_grads(0, dz0, False)

    def copy_a(j):
        peer = lax.rem(cs + j, ncs)
        return pltpu.make_async_remote_copy(
            src_ref=acc_ref.at[pl.ds(pl.multiple_of(peer * chunk_rows, 8), chunk_rows), :],
            dst_ref=rcv_a.at[j], send_sem=sa_send.at[j], recv_sem=sa_recv.at[j],
            device_id=dev(al, peer), device_id_type=MESH,
        )

    def copy_b(j):
        return pltpu.make_async_remote_copy(
            src_ref=src_b, dst_ref=rcv_b.at[al], send_sem=sb_send.at[j], recv_sem=sb_recv.at[j],
            device_id=dev(lax.rem(al + j, nal), cs), device_id_type=MESH,
        )

    mine = pl.ds(pl.multiple_of(cs * chunk_rows, 8), chunk_rows)

    def copy_c(j):
        return pltpu.make_async_remote_copy(
            src_ref=full_ref.at[mine, :], dst_ref=full_ref.at[mine, :],
            send_sem=sc_send.at[j], recv_sem=sc_recv.at[j],
            device_id=dev(al, lax.rem(cs + j, ncs)), device_id_type=MESH,
        )

    for j in range(1, ncs):
        copy_a(j).start()
    finish(3)
    last = gather(c0, to0, 3)
    for f in range(12):
        gstate_ref[f] = last[f]
    total = acc_ref[mine, :]
    for j in range(1, ncs):
        copy_a(j).wait_recv()
        total = total + rcv_a[j]
    src_b[...] = total
    rcv_b[al] = total
    for j in range(1, nal):
        copy_b(j).start()
    for j in range(1, nal):
        copy_b(j).wait_recv()
    total = rcv_b[0]
    for j in range(1, nal):
        total = total + rcv_b[j]
    full_ref[mine, :] = total * factor
    for j in range(1, ncs):
        copy_c(j).start()
    for j in range(1, ncs):
        copy_c(j).wait_recv()
    gw1_ref[...] = full_ref[0:32, :]
    gb1_ref[...] = full_ref[ROW_B1:ROW_B1 + 1, :]
    gw2_ref[...] = full_ref[ROW_W2:ROW_W2 + 128, :]
    gb2_ref[...] = full_ref[ROW_B2:ROW_B2 + 1, :]
    tail = jnp.concatenate([full_ref[ROW_WO:ROW_BO + 8, :], jnp.zeros((112, 128), f32)], axis=0)
    turned = jnp.transpose(tail)
    gwo_ref[...] = turned[:, :8]
    gbo_ref[...] = turned[0:1, 8:16]
    for k in range(4):
        finish_sends(k)
    for j in range(1, ncs):
        copy_a(j).wait_send()
        copy_c(j).wait_send()
    for j in range(1, nal):
        copy_b(j).wait_send()


def solution(mesh):
    nal, ncr, nsu = mesh.shape["along"], mesh.shape["cross"], mesh.shape["sub"]
    ncs = ncr * nsu
    chunk_rows = 8 * (-(-PACK_ROWS // (8 * ncs)))
    total_rows = chunk_rows * ncs

    def per_device(state, storm, wet, dune, cid, w1, b1, w2, b2, wo, bo, cot):
        rows, cols = state.shape[1], state.shape[2]
        factor = 1.0 / math.sqrt(rows * nal * cols * ncs)
        vmem = pl.BlockSpec(memory_space=pltpu.VMEM)
        smem = pl.BlockSpec(memory_space=pltpu.SMEM)
        dma = pltpu.SemaphoreType.DMA
        big = lambda n, kind: pltpu.VMEM((2, n, 1024), kind)
        out = pl.pallas_call(
            functools.partial(kernel, nal, ncr, nsu, chunk_rows, factor),
            out_shape=(
                jax.ShapeDtypeStruct((12, 8, 128), f32),
                jax.ShapeDtypeStruct((32, 128), f32),
                jax.ShapeDtypeStruct((1, 128), f32),
                jax.ShapeDtypeStruct((128, 128), f32),
                jax.ShapeDtypeStruct((1, 128), f32),
                jax.ShapeDtypeStruct((128, 8), f32),
                jax.ShapeDtypeStruct((1, 8), f32),
            ),
            in_specs=[vmem] * 10 + [smem, vmem],
            out_specs=(vmem,) * 7,
            scratch_shapes=[
                pltpu.VMEM((4, 2, 16, 128), f32),
                pltpu.VMEM((4, 2, 8, 128), f32),
                pltpu.VMEM((4, 2, 16, 128), f32),
                pltpu.VMEM((4, 2, 8, 128), f32),
                dma((4, 4)), dma((4, 4)),
                pltpu.VMEM((256, 128), f32),
                pltpu.VMEM((256, 128), f32),
                pltpu.VMEM((8, 128), f32),
                pltpu.VMEM((8, 128), f32),
                pltpu.VMEM((128, 128), f32),
                pltpu.VMEM((128, 128), f32),
                pltpu.VMEM((128, 1024), f32),
                big(32, bf16), big(32, bf16), big(128, bf16), big(128, bf16), big(128, bf16), big(128, bf16),
                big(128, f32), big(128, f32), big(128, bf16), big(128, bf16), big(128, bf16), big(128, bf16),
                pltpu.VMEM((16, 1024), bf16), pltpu.VMEM((16, 1024), bf16),
                pltpu.VMEM((total_rows, 128), f32),
                pltpu.VMEM((ncs, chunk_rows, 128), f32),
                pltpu.VMEM((chunk_rows, 128), f32),
                pltpu.VMEM((nal, chunk_rows, 128), f32),
                pltpu.VMEM((total_rows, 128), f32),
                dma((ncs,)), dma((ncs,)), dma((nal,)), dma((nal,)), dma((ncs,)), dma((ncs,)),
            ],
            compiler_params=pltpu.CompilerParams(collective_id=0, has_side_effects=True),
        )(state, storm, wet, dune, cid, w1, b1.reshape(1, 128), w2, b2.reshape(1, 128), wo, bo, cot)
        gs, gw1, gb1, gw2, gb2, gwo, gbo = out
        return gs, gw1, gb1.reshape(128), gw2, gb2.reshape(128), gwo, gbo.reshape(8)

    tile = P(None, ("groups", "along"), ("cross", "sub"))
    return jax.shard_map(
        per_device,
        mesh=mesh,
        in_specs=(
            tile, tile, tile, tile, P(("groups", "along"), ("cross", "sub")),
            P(), P(), P(), P(), P(), P(), tile,
        ),
        out_specs=(
            tile, P("groups", None), P("groups"), P("groups", None), P("groups"),
            P("groups", None), P("groups"),
        ),
        check_vma=False,
    )
```

time: 235 us -> 37.4 us (0.16)
  waiting for transfers between devices: 69.5 us -> 0 us
  blocking collectives: 64.9 us -> 0 us
  starting transfers between devices: 44.2 us -> 0 us
  Pallas kernels: 0 us -> 29.8 us
  between operations: 15 us -> 0.66 us
  matrix products: 13.8 us -> 0 us
  other arithmetic: 11.8 us -> 0 us
  local copies, waits for them, and re-layouts: 13.7 us -> 6.62 us
    psum x1 -> x0, blocking collectives: 64.9 us -> none  [sum_once(): lax.psum((grads[0], grads[1], grads[2], grads[3], grads[4], grads[5]), ('...]
    psum x1 -> x0, waiting for transfers between devices: 64.1 us -> none  [sum_once(): lax.psum((grads[0], grads[1], grads[2], grads[3], grads[4], grads[5]), ('...]
    ppermute x16 -> x0, starting transfers between devices: 44.2 us -> none  [the longest x8 33.7 us: with_halo(): lax.ppermute(lax.slice_in_dim(block, block.shape[dim] - width, None, axis...]
    pallas_call x0 -> x1, Pallas kernels: none -> 29.8 us  [per_device(): pl.pallas_call(functools.partial(kernel, nal, ncr, nsu, chunk_rows, facto...]
    dot_general x18 -> x0, matrix products: 13.8 us -> none  [the longest x6 5.42 us: layer_stack(): jnp.einsum('hk,hrc->krc', w_two, hidden_one, precision=highest)]
    scatter-add x16 -> x0, local copies, waits for them, and re-layouts: 9.08 us -> none  [the longest x2 4.26 us: fold_rims(): interior.at[:, :rim_width, -rim_width:]]
    ppermute x16 -> x0, waiting for transfers between devices: 5.4 us -> none  [the longest x8 3.64 us: with_halo(): lax.ppermute(lax.slice_in_dim(block, block.shape[dim] - width, None, axis...]
    unnamed x32 -> x20, local copies, waits for them, and re-layouts: 1.89 us -> 6.62 us
  transfers between devices with their start and end apart: 17 -> 0, of which waited for: 8 -> 0; matrix products, arithmetic and copies ran while one was open for 5% -> 0% of each run, Pallas kernels for 0% -> 0%
where the time goes in v1:
time: 37.4 us; the launch traced here: 37.1 us
  Pallas kernels  29.8 us (80%)
  local copies, waits for them, and re-layouts  6.62 us (18%)
  between operations  0.66 us (2%)
    pallas_call x1, Pallas kernels, per_device(): pl.pallas_call(functools.partial(kernel, nal, ncr, nsu, chunk_rows, facto...  29.8 us
    unnamed x20, local copies, waits for them, and re-layouts  6.62 us

profile of v1, /device:TPU:0, one launch (start us, length us, event | category | flops | bytes accessed | tf_op | source)
XLA Modules:
  0.0 37.1 jit_solution(11943950208707093957)
XLA Ops:
  0.6 1.4 %copy.19.wo_ref = f32[128,8]{1,0:T(8,128)} copy(f32[128,8]{0,1:T(8,128)} %param.21) | data formatting | bytes 8192 | tf_op args[9]
  2.0 29.8 %shard_map.171 = (f32[12,8,128]{2,1,0:T(8,128)}, f32[32,128]{1,0:T(8,128)}, f32[1,128]{1,0:T(1,128)}, f32[128,128]{1,0:T(8,128)}, f32[1,128]{1,0:T(1,128)}, /*index=5*/f32[128,8]{1,0:T(8,128)}, f32[1,8]{1,0:T(1,128)}) custom-call(f32[12,8,128]{2,1,0:T(8,128)} %state_ref.1, f32[12,8,128]{2,1,0:T(8,128)} %storm_ref.1, s32[2,8,128]{2,1,0:T(8,128)} %wet_ref.1, ...), custom_call_target="tpu_custom_call" | custom-call | tf_op jit(solution)/shard_map/pallas_call | solution.py:430
  31.8 0.0 copy-start.1
  31.8 1.5 %copy.20 = f32[128,8]{0,1:T(8,128)} copy(f32[128,8]{1,0:T(8,128)} %get-tuple-element.26) | data formatting | bytes 8192
  33.4 0.0 copy-done.1
  33.4 0.0 copy-start.2
  33.4 0.0 copy-start
  33.4 0.6 %copy.27 = f32[12,8,128]{2,1,0:T(8,128)} copy(f32[12,8,128]{2,1,0:T(8,128)S(1)} %copy-done.1) | data formatting | bytes 98304
  34.0 0.1 copy-done.2
  34.1 0.0 copy-start.5
  34.1 0.6 %copy.28 = f32[32,128]{1,0:T(8,128)} copy(f32[32,128]{1,0:T(8,128)S(1)} %copy-done.2) | data formatting | bytes 32768
  34.7 0.1 copy-done.5
  34.8 0.5 %copy.29 = f32[128]{0:T(128)} copy(f32[128]{0:T(128)S(1)} %bitcast.9) | data formatting | bytes 1024
  35.3 0.0 copy-done
  35.3 0.0 copy-start.4
  35.3 0.6 %copy.30 = f32[128,128]{1,0:T(8,128)} copy(f32[128,128]{1,0:T(8,128)S(1)} %copy-done) | data formatting | bytes 131072
  35.9 0.0 copy-done.4
  35.9 0.0 copy-start.3
  35.9 0.5 %copy.31 = f32[128]{0:T(128)} copy(f32[128]{0:T(128)S(1)} %bitcast.8) | data formatting | bytes 1024
  36.5 0.1 copy-done.3
  36.5 0.5 %copy.32 = f32[8]{0:T(128)} copy(f32[8]{0:T(128)S(1)} %bitcast.7) | data formatting | bytes 64
Async XLA Ops:
  31.8 1.5 %copy-start.1 = (f32[12,8,128]{2,1,0:T(8,128)S(1)}, f32[12,8,128]{2,1,0:T(8,128)}, u32[]{:S(2)}) copy-start(f32[12,8,128]{2,1,0:T(8,128)} %get-tuple-element.35) | copy-start | bytes 147460
  33.4 0.7 %copy-start.2 = (f32[32,128]{1,0:T(8,128)S(1)}, f32[32,128]{1,0:T(8,128)}, u32[]{:S(2)}) copy-start(f32[32,128]{1,0:T(8,128)} %get-tuple-element.36) | copy-start | bytes 49156
  33.4 1.9 %copy-start = (f32[128,128]{1,0:T(8,128)S(1)}, f32[128,128]{1,0:T(8,128)}, u32[]{:S(2)}) copy-start(f32[128,128]{1,0:T(8,128)} %get-tuple-element.38) | copy-start | bytes 196612
  34.1 0.7 %copy-start.5 = (f32[1,128]{1,0:T(1,128)S(1)}, f32[1,128]{1,0:T(1,128)}, u32[]{:S(2)}) copy-start(f32[1,128]{1,0:T(1,128)} %get-tuple-element.16) | copy-start | bytes 1540
  35.3 0.7 %copy-start.4 = (f32[1,128]{1,0:T(1,128)S(1)}, f32[1,128]{1,0:T(1,128)}, u32[]{:S(2)}) copy-start(f32[1,128]{1,0:T(1,128)} %get-tuple-element.18) | copy-start | bytes 1540
  35.9 0.6 %copy-start.3 = (f32[1,8]{1,0:T(1,128)S(1)}, f32[1,8]{1,0:T(1,128)}, u32[]{:S(2)}) copy-start(f32[1,8]{1,0:T(1,128)} %get-tuple-element.20) | copy-start | bytes 100

commit v2 on v1

--- a/solution.py
+++ b/solution.py
@@ -19,11 +19,11 @@
 bed_diffusion = 0.1
 
 ROW_B1 = 32
-ROW_W2 = 40
-ROW_B2 = 168
-ROW_WO = 176
-ROW_BO = 184
-PACK_ROWS = 192
+ROWS_ONE = 40
+ROW_B2 = 128
+ROW_WO = 136
+ROW_BO = 144
+ROWS_TWO = 152
 LANES = 256
 CHUNKS = 4
 
@@ -43,16 +43,17 @@
 
 
 def kernel(
-    nal, ncr, nsu, chunk_rows, factor,
+    nal, ncr, nsu, factor,
     state_ref, storm_ref, wet_ref, dune_ref, cid_ref,
     w1_ref, b1_ref, w2_ref, b2_ref, wo_ref, bo_ref, cot_ref,
-    gstate_ref, gw1_ref, gb1_ref, gw2_ref, gb2_ref, gwo_ref, gbo_ref,
+    gstate_ref, full_one, full_two,
     snd_row, snd_col, rcv_row, rcv_col, send_sem, recv_sem,
     feat_ref, dfeat_ref, z_ref, dz_ref,
     b1b_ref, b2b_ref, wsel_ref,
     fh_ref, fl_ref, h1h_ref, h1l_ref, h2h_ref, h2l_ref,
     act1_ref, q2_ref, d1h_ref, d1l_ref, d2h_ref, d2l_ref, drh_ref, drl_ref,
-    acc_ref, rcv_a, src_b, rcv_b, full_ref,
+    acc_one, rcv_a_one, src_b_one, rcv_b_one, dst_one,
+    acc_two, rcv_a_two, src_b_two, rcv_b_two, dst_two,
     sa_send, sa_recv, sb_send, sb_recv, sc_send, sc_recv,
 ):
     ncs = ncr * nsu
@@ -159,10 +160,11 @@
     b2b_ref[...] = jnp.transpose(jnp.broadcast_to(b2_ref[...], (128, 128)))
     cid = cid_ref[...]
     wo = wo_ref[...]
+    wo_t = jnp.transpose(jnp.concatenate([wo, jnp.zeros((120, 128), f32)], axis=0))[:, :8]
     for r in range(8):
         onehot = (lax.broadcasted_iota(jnp.int32, (8, 128), 0) == cid[r:r + 1, :]).astype(f32)
         wsel_ref[:, r * 128:(r + 1) * 128] = lax.dot_general(
-            wo, onehot, (((1,), (0,)), ((), ())),
+            wo_t, onehot, (((1,), (0,)), ((), ())),
             precision=lax.Precision.HIGHEST, preferred_element_type=f32,
         )
     bsel = jnp.zeros((8, 128), f32)
@@ -217,7 +219,7 @@
                 z_ref[2 * c + i:2 * c + i + 1, :] = z[:, i * 128:(i + 1) * 128]
         return near, z_ref[...] + bsel
 
-    def backward(t, z, near, V, lam):
+    def adjoint_two(t, z, lam):
         G = [wets[t] * lam[f] for f in range(12)]
         picked = G[4]
         for k in range(1, 8):
@@ -230,15 +232,24 @@
             drow = jnp.concatenate(
                 [dz_ref[2 * c + i:2 * c + i + 1, :] for i in range(2)], axis=1
             )
-            d2 = q2_ref[t, :, at] * drow
-            Dh, Dl = split(d2)
+            Dh, Dl = split(q2_ref[t, :, at] * drow)
             d2h_ref[t, :, at] = Dh
             d2l_ref[t, :, at] = Dl
+        return G, dz
+
+    def adjoint_one(t):
+        for c in range(CHUNKS):
+            at = pl.ds(c * LANES, LANES)
+            Dh, Dl = d2h_ref[t, :, at], d2l_ref[t, :, at]
             d1 = mm(w2_hh, jnp.concatenate([Dh, Dl], axis=0)) + mm(w2l, Dh)
-            d1 = d1 * act1_ref[t, :, at]
-            Dh, Dl = split(d1)
+            Dh, Dl = split(d1 * act1_ref[t, :, at])
             d1h_ref[t, :, at] = Dh
             d1l_ref[t, :, at] = Dl
+
+    def adjoint_cells(t, G, near, V, lam):
+        for c in range(CHUNKS):
+            at = pl.ds(c * LANES, LANES)
+            Dh, Dl = d1h_ref[t, :, at], d1l_ref[t, :, at]
             dF = mm(w1_hh, jnp.concatenate([Dh, Dl], axis=0)) + mm(w1l, Dh)
             for i in range(2):
                 dfeat_ref[pl.ds(2 * c + i, 32, stride=8), :] = dF[:, i * 128:(i + 1) * 128]
@@ -271,7 +282,7 @@
                 to[d].append(x)
             if f < 4:
                 c[f] = c[f] + D[f]
-        return dz, c, to
+        return c, to
 
     def gather(c, to, k):
         return [
@@ -280,8 +291,11 @@
             for f in range(12)
         ]
 
-    def weight_grads(t, dz, first):
-        ones = jnp.ones((16, 1024), bf16)
+    def keep(ref, start, part, first):
+        at = pl.ds(start, part.shape[0])
+        ref[at, :] = part if first else ref[at, :] + part
+
+    def weights_two(t, dz, first):
         chooser_rows = []
         for r in range(8):
             onehot = lax.broadcasted_iota(jnp.int32, (8, 128), 0) == cid[r:r + 1, :]
@@ -290,22 +304,22 @@
         dbo = jnp.broadcast_to(jnp.sum(dr, axis=1, keepdims=True), (8, 128))
         pad = jnp.zeros((8, 1024), f32)
         drh, drl = split(jnp.concatenate([dr, pad], axis=0))
-        h2h, h2l = h2h_ref[t], h2l_ref[t]
-        top = mm_nt(jnp.concatenate([drh, drl], axis=0), h2h)
-        dwo = top[:8] + top[16:24] + mm_nt(drh, h2l)[:8]
-        lhs = jnp.concatenate([h1h_ref[t], ones, h1l_ref[t]], axis=0)
+        top = mm_nt(jnp.concatenate([drh, drl], axis=0), h2h_ref[t])
+        dwo = top[:8] + top[16:24] + mm_nt(drh, h2l_ref[t])[:8]
+        lhs = jnp.concatenate([h1h_ref[t], jnp.ones((16, 1024), bf16), h1l_ref[t]], axis=0)
         top = mm_nt(lhs, d2h_ref[t])
         low = mm_nt(lhs[:144], d2l_ref[t])
-        dw2 = top[:128] + top[144:272] + low[:128]
-        db2 = top[128:136] + low[128:136]
-        lhs = jnp.concatenate([fh_ref[t], ones, fl_ref[t]], axis=0)
+        keep(acc_two, 0, top[:128] + top[144:272] + low[:128], first)
+        keep(acc_two, ROW_B2, top[128:136] + low[128:136], first)
+        keep(acc_two, ROW_WO, dwo, first)
+        keep(acc_two, ROW_BO, dbo, first)
+
+    def weights_one(t, first):
+        lhs = jnp.concatenate([fh_ref[t], jnp.ones((16, 1024), bf16), fl_ref[t]], axis=0)
         top = mm_nt(lhs, d1h_ref[t])
         low = mm_nt(lhs[:48], d1l_ref[t])
-        dw1 = top[:32] + top[48:80] + low[:32]
-        db1 = top[32:40] + low[32:40]
-        for start, part in ((0, dw1), (ROW_B1, db1), (ROW_W2, dw2), (ROW_B2, db2), (ROW_WO, dwo), (ROW_BO, dbo)):
-            at = pl.ds(start, part.shape[0])
-            acc_ref[at, :] = part if first else acc_ref[at, :] + part
+        keep(acc_one, 0, top[:32] + top[48:80] + low[:32], first)
+        keep(acc_one, ROW_B1, top[32:40] + low[32:40], first)
 
     finish(0)
     near0, z0 = forward(0, V0, 0)
@@ -338,87 +352,130 @@
 
     near1, z1 = forward(1, V1, 1)
     lam2 = [cot_ref[f] for f in range(12)]
-    dz1, c1, to1 = backward(1, z1, near1, V1, lam2)
+    G1, dz1 = adjoint_two(1, z1, lam2)
+    adjoint_one(1)
+    c1, to1 = adjoint_cells(1, G1, near1, V1, lam2)
     fill(2, *to1)
     launch(2)
-    weight_grads(1, dz1, True)
+    for ref, used in ((acc_one, ROWS_ONE), (acc_two, ROWS_TWO)):
+        if ref.shape[0] > used:
+            ref[used:, :] = jnp.zeros((ref.shape[0] - used, 128), f32)
+    weights_two(1, dz1, True)
+    weights_one(1, True)
     finish(2)
     lam1 = gather(c1, to1, 2)
 
-    dz0, c0, to0 = backward(0, z0, near0, V0, lam1)
+    class Sum:
+        def __init__(self, which, acc, rcv_a, src_b, rcv_b, full):
+            self.which, self.acc, self.rcv_a, self.src_b = which, acc, rcv_a, src_b
+            self.rcv_b, self.full = rcv_b, full
+            self.rows = src_b.shape[0]
+            self.mine = pl.ds(pl.multiple_of(cs * self.rows, 8), self.rows)
+
+        def copy_a(self, j):
+            peer = lax.rem(cs + j, ncs)
+            return pltpu.make_async_remote_copy(
+                src_ref=self.acc.at[pl.ds(pl.multiple_of(peer * self.rows, 8), self.rows), :],
+                dst_ref=self.rcv_a.at[j],
+                send_sem=sa_send.at[self.which, j], recv_sem=sa_recv.at[self.which, j],
+                device_id=dev(al, peer), device_id_type=MESH,
+            )
+
+        def copy_b(self, j):
+            return pltpu.make_async_remote_copy(
+                src_ref=self.src_b, dst_ref=self.rcv_b.at[al],
+                send_sem=sb_send.at[self.which, j], recv_sem=sb_recv.at[self.which, j],
+                device_id=dev(lax.rem(al + j, nal), cs), device_id_type=MESH,
+            )
+
+        def copy_c(self, j):
+            return pltpu.make_async_remote_copy(
+                src_ref=self.full.at[self.mine, :], dst_ref=self.full.at[self.mine, :],
+                send_sem=sc_send.at[self.which, j], recv_sem=sc_recv.at[self.which, j],
+                device_id=dev(al, lax.rem(cs + j, ncs)), device_id_type=MESH,
+            )
+
+        def first(self):
+            for j in range(1, ncs):
+                self.copy_a(j).start()
+
+        def second(self):
+            total = self.acc[self.mine, :]
+            for j in range(1, ncs):
+                self.copy_a(j).wait_recv()
+                total = total + self.rcv_a[j]
+            self.src_b[...] = total
+            self.rcv_b[al] = total
+            for j in range(1, nal):
+                self.copy_b(j).start()
+
+        def third(self):
+            for j in range(1, nal):
+                self.copy_b(j).wait_recv()
+            total = self.rcv_b[0]
+            for j in range(1, nal):
+                total = total + self.rcv_b[j]
+            self.full[self.mine, :] = total * factor
+            for j in range(1, ncs):
+                self.copy_c(j).start()
+
+        def fourth(self):
+            for j in range(1, ncs):
+                self.copy_c(j).wait_recv()
+
+        def sends(self):
+            for j in range(1, ncs):
+                self.copy_a(j).wait_send()
+                self.copy_c(j).wait_send()
+            for j in range(1, nal):
+                self.copy_b(j).wait_send()
+
+    sum_two = Sum(0, acc_two, rcv_a_two, src_b_two, rcv_b_two, dst_two)
+    sum_one = Sum(1, acc_one, rcv_a_one, src_b_one, rcv_b_one, dst_one)
+
+    G0, dz0 = adjoint_two(0, z0, lam1)
+    weights_two(0, dz0, False)
+    sum_two.first()
+    adjoint_one(0)
+    weights_one(0, False)
+    sum_one.first()
+    sum_two.second()
+    c0, to0 = adjoint_cells(0, G0, near0, V0, lam1)
     fill(3, *to0)
     launch(3)
-    weight_grads(0, dz0, False)
-
-    def copy_a(j):
-        peer = lax.rem(cs + j, ncs)
-        return pltpu.make_async_remote_copy(
-            src_ref=acc_ref.at[pl.ds(pl.multiple_of(peer * chunk_rows, 8), chunk_rows), :],
-            dst_ref=rcv_a.at[j], send_sem=sa_send.at[j], recv_sem=sa_recv.at[j],
-            device_id=dev(al, peer), device_id_type=MESH,
-        )
-
-    def copy_b(j):
-        return pltpu.make_async_remote_copy(
-            src_ref=src_b, dst_ref=rcv_b.at[al], send_sem=sb_send.at[j], recv_sem=sb_recv.at[j],
-            device_id=dev(lax.rem(al + j, nal), cs), device_id_type=MESH,
-        )
-
-    mine = pl.ds(pl.multiple_of(cs * chunk_rows, 8), chunk_rows)
-
-    def copy_c(j):
-        return pltpu.make_async_remote_copy(
-            src_ref=full_ref.at[mine, :], dst_ref=full_ref.at[mine, :],
-            send_sem=sc_send.at[j], recv_sem=sc_recv.at[j],
-            device_id=dev(al, lax.rem(cs + j, ncs)), device_id_type=MESH,
-        )
-
-    for j in range(1, ncs):
-        copy_a(j).start()
+    sum_one.second()
+    sum_two.third()
     finish(3)
     last = gather(c0, to0, 3)
     for f in range(12):
         gstate_ref[f] = last[f]
-    total = acc_ref[mine, :]
-    for j in range(1, ncs):
-        copy_a(j).wait_recv()
-        total = total + rcv_a[j]
-    src_b[...] = total
-    rcv_b[al] = total
-    for j in range(1, nal):
-        copy_b(j).start()
-    for j in range(1, nal):
-        copy_b(j).wait_recv()
-    total = rcv_b[0]
-    for j in range(1, nal):
-        total = total + rcv_b[j]
-    full_ref[mine, :] = total * factor
-    for j in range(1, ncs):
-        copy_c(j).start()
-    for j in range(1, ncs):
-        copy_c(j).wait_recv()
-    gw1_ref[...] = full_ref[0:32, :]
-    gb1_ref[...] = full_ref[ROW_B1:ROW_B1 + 1, :]
-    gw2_ref[...] = full_ref[ROW_W2:ROW_W2 + 128, :]
-    gb2_ref[...] = full_ref[ROW_B2:ROW_B2 + 1, :]
-    tail = jnp.concatenate([full_ref[ROW_WO:ROW_BO + 8, :], jnp.zeros((112, 128), f32)], axis=0)
-    turned = jnp.transpose(tail)
-    gwo_ref[...] = turned[:, :8]
-    gbo_ref[...] = turned[0:1, 8:16]
+    sum_one.third()
+    sum_two.fourth()
+    full_two[...] = dst_two[...]
+    sum_one.fourth()
+    full_one[...] = dst_one[...]
     for k in range(4):
         finish_sends(k)
-    for j in range(1, ncs):
-        copy_a(j).wait_send()
-        copy_c(j).wait_send()
-    for j in range(1, nal):
-        copy_b(j).wait_send()
+    sum_two.sends()
+    sum_one.sends()
+
+
+def unpack(state_ref, one_ref, two_ref, gs_ref, gw1_ref, gb1_ref, gw2_ref, gb2_ref, gwo_ref, gbo_ref):
+    gs_ref[...] = state_ref[...]
+    gw1_ref[...] = one_ref[0:32, :]
+    gb1_ref[...] = one_ref[ROW_B1:ROW_B1 + 1, :]
+    gw2_ref[...] = two_ref[0:128, :]
+    gb2_ref[...] = two_ref[ROW_B2:ROW_B2 + 1, :]
+    gwo_ref[...] = two_ref[ROW_WO:ROW_WO + 8, :]
+    wide = jnp.concatenate([two_ref[ROW_BO:ROW_BO + 8, :], jnp.zeros((120, 128), f32)], axis=0)
+    gbo_ref[...] = jnp.transpose(wide)[0:1, :8]
 
 
 def solution(mesh):
     nal, ncr, nsu = mesh.shape["along"], mesh.shape["cross"], mesh.shape["sub"]
     ncs = ncr * nsu
-    chunk_rows = 8 * (-(-PACK_ROWS // (8 * ncs)))
-    total_rows = chunk_rows * ncs
+    rows_one = 8 * (-(-ROWS_ONE // (8 * ncs)))
+    rows_two = 8 * (-(-ROWS_TWO // (8 * ncs)))
 
     def per_device(state, storm, wet, dune, cid, w1, b1, w2, b2, wo, bo, cot):
         rows, cols = state.shape[1], state.shape[2]
@@ -427,19 +484,22 @@
         smem = pl.BlockSpec(memory_space=pltpu.SMEM)
         dma = pltpu.SemaphoreType.DMA
         big = lambda n, kind: pltpu.VMEM((2, n, 1024), kind)
+        summed = lambda n: [
+            pltpu.VMEM((ncs * n, 128), f32),
+            pltpu.VMEM((ncs, n, 128), f32),
+            pltpu.VMEM((n, 128), f32),
+            pltpu.VMEM((nal, n, 128), f32),
+            pltpu.VMEM((ncs * n, 128), f32),
+        ]
         out = pl.pallas_call(
-            functools.partial(kernel, nal, ncr, nsu, chunk_rows, factor),
+            functools.partial(kernel, nal, ncr, nsu, factor),
             out_shape=(
                 jax.ShapeDtypeStruct((12, 8, 128), f32),
-                jax.ShapeDtypeStruct((32, 128), f32),
-                jax.ShapeDtypeStruct((1, 128), f32),
-                jax.ShapeDtypeStruct((128, 128), f32),
-                jax.ShapeDtypeStruct((1, 128), f32),
-                jax.ShapeDtypeStruct((128, 8), f32),
-                jax.ShapeDtypeStruct((1, 8), f32),
+                jax.ShapeDtypeStruct((ncs * rows_one, 128), f32),
+                jax.ShapeDtypeStruct((ncs * rows_two, 128), f32),
             ),
             in_specs=[vmem] * 10 + [smem, vmem],
-            out_specs=(vmem,) * 7,
+            out_specs=(vmem,) * 3,
             scratch_shapes=[
                 pltpu.VMEM((4, 2, 16, 128), f32),
                 pltpu.VMEM((4, 2, 8, 128), f32),
@@ -456,17 +516,27 @@
                 big(32, bf16), big(32, bf16), big(128, bf16), big(128, bf16), big(128, bf16), big(128, bf16),
                 big(128, f32), big(128, f32), big(128, bf16), big(128, bf16), big(128, bf16), big(128, bf16),
                 pltpu.VMEM((16, 1024), bf16), pltpu.VMEM((16, 1024), bf16),
-                pltpu.VMEM((total_rows, 128), f32),
-                pltpu.VMEM((ncs, chunk_rows, 128), f32),
-                pltpu.VMEM((chunk_rows, 128), f32),
-                pltpu.VMEM((nal, chunk_rows, 128), f32),
-                pltpu.VMEM((total_rows, 128), f32),
-                dma((ncs,)), dma((ncs,)), dma((nal,)), dma((nal,)), dma((ncs,)), dma((ncs,)),
+                *summed(rows_one), *summed(rows_two),
+                dma((2, ncs)), dma((2, ncs)), dma((2, nal)), dma((2, nal)), dma((2, ncs)), dma((2, ncs)),
             ],
             compiler_params=pltpu.CompilerParams(collective_id=0, has_side_effects=True),
-        )(state, storm, wet, dune, cid, w1, b1.reshape(1, 128), w2, b2.reshape(1, 128), wo, bo, cot)
-        gs, gw1, gb1, gw2, gb2, gwo, gbo = out
-        return gs, gw1, gb1.reshape(128), gw2, gb2.reshape(128), gwo, gbo.reshape(8)
+        )(state, storm, wet, dune, cid, w1, b1.reshape(1, 128), w2, b2.reshape(1, 128), wo.T, bo, cot)
+        gs, gw1, gb1, gw2, gb2, gwo, gbo = pl.pallas_call(
+            unpack,
+            out_shape=(
+                jax.ShapeDtypeStruct((12, 8, 128), f32),
+                jax.ShapeDtypeStruct((32, 128), f32),
+                jax.ShapeDtypeStruct((1, 128), f32),
+                jax.ShapeDtypeStruct((128, 128), f32),
+                jax.ShapeDtypeStruct((1, 128), f32),
+                jax.ShapeDtypeStruct((8, 128), f32),
+                jax.ShapeDtypeStruct((1, 8), f32),
+            ),
+            in_specs=[vmem] * 3,
+            out_specs=(vmem,) * 7,
+            compiler_params=pltpu.CompilerParams(vmem_limit_bytes=4 << 20),
+        )(*out)
+        return gs, gw1, gb1.reshape(128), gw2, gb2.reshape(128), gwo.T, gbo.reshape(8)
 
     tile = P(None, ("groups", "along"), ("cross", "sub"))
     return jax.shard_map(

time: 37.4 us -> 34 us (0.909)
  local copies, waits for them, and re-layouts: 6.62 us -> 2.44 us
  Pallas kernels: 29.8 us -> 30.5 us
    unnamed x20 -> x6, local copies, waits for them, and re-layouts: 6.62 us -> 2.44 us
    pallas_call x1 -> x2, Pallas kernels: 29.8 us -> 30.5 us  [the longest x1 29.9 us: per_device(): pl.pallas_call(functools.partial(kernel, nal, ncr, nsu, factor), out_shap...]
where the time goes in v2:
time: 34 us; the launch traced here: 33.6 us
  Pallas kernels  30.5 us (90%)
  local copies, waits for them, and re-layouts  2.44 us (7%)
  between operations  0.66 us (2%)
    pallas_call x1, Pallas kernels, per_device(): pl.pallas_call(functools.partial(kernel, nal, ncr, nsu, factor), out_shap...  29.9 us
    unnamed x6, local copies, waits for them, and re-layouts  2.44 us

profile of v2, /device:TPU:0, one launch (start us, length us, event | category | flops | bytes accessed | tf_op | source)
XLA Modules:
  0.0 33.6 jit_solution(9838612919240685302)
XLA Ops:
  0.6 29.9 %shard_map.171 = (f32[12,8,128]{2,1,0:T(8,128)}, f32[64,128]{1,0:T(8,128)}, f32[160,128]{1,0:T(8,128)}) custom-call(f32[12,8,128]{2,1,0:T(8,128)} %state_ref.1, f32[12,8,128]{2,1,0:T(8,128)} %storm_ref.1, s32[2,8,128]{2,1,0:T(8,128)} %wet_ref.1, s32[2,8,128]{2,1,0:T(8,128)} %dune_ref.1, s32[8,128]{1,0:T(8,128)} %cid_ref.1, f32[32,128]{1,0:T(8,128)} %w1_ref.1, ...), custom_call_target="tpu_custom_call" | custom-call | tf_op jit(solution)/shard_map/pallas_call | solution.py:494
  30.5 0.0 copy-start
  30.5 0.9 %copy-done = f32[160,128]{1,0:T(8,128)S(1)} copy-done((f32[160,128]{1,0:T(8,128)S(1)}, f32[160,128]{1,0:T(8,128)}, u32[]{:S(2)}) %copy-start) | copy-done | bytes 81944
  31.4 0.0 copy-start.1
  31.4 0.8 %copy-done.1 = f32[12,8,128]{2,1,0:T(8,128)S(1)} copy-done((f32[12,8,128]{2,1,0:T(8,128)S(1)}, f32[12,8,128]{2,1,0:T(8,128)}, u32[]{:S(2)}) %copy-start.1) | copy-done | bytes 49176
  32.2 0.0 copy-start.2
  32.2 0.8 %copy-done.2 = f32[64,128]{1,0:T(8,128)S(1)} copy-done((f32[64,128]{1,0:T(8,128)S(1)}, f32[64,128]{1,0:T(8,128)}, u32[]{:S(2)}) %copy-start.2) | copy-done | bytes 32792
  33.0 0.7 %shard_map.172 = (f32[12,8,128]{2,1,0:T(8,128)}, f32[32,128]{1,0:T(8,128)}, f32[1,128]{1,0:T(1,128)}, f32[128,128]{1,0:T(8,128)}, f32[1,128]{1,0:T(1,128)}, /*index=5*/f32[8,128]{1,0:T(8,128)}, f32[1,8]{1,0:T(1,128)}) custom-call(f32[12,8,128]{2,1,0:T(8,128)S(1)} %copy-done.1, f32[64,128]{1,0:T(8,128)S(1)} %copy-done.2, f32[160,128]{1,0:T(8,128)S(1)} %copy-done), custom_call_target="tpu_custom_call" | custom-call | tf_op jit(solution)/shard_map/pallas_call | solution.py:524
Async XLA Ops:
  30.5 0.9 %copy-start = (f32[160,128]{1,0:T(8,128)S(1)}, f32[160,128]{1,0:T(8,128)}, u32[]{:S(2)}) copy-start(f32[160,128]{1,0:T(8,128)} %get-tuple-element.19.two_ref) | copy-start | bytes 245764
  31.4 0.8 %copy-start.1 = (f32[12,8,128]{2,1,0:T(8,128)S(1)}, f32[12,8,128]{2,1,0:T(8,128)}, u32[]{:S(2)}) copy-start(f32[12,8,128]{2,1,0:T(8,128)} %get-tuple-element.17.state_ref) | copy-start | bytes 147460
  32.2 0.8 %copy-start.2 = (f32[64,128]{1,0:T(8,128)S(1)}, f32[64,128]{1,0:T(8,128)}, u32[]{:S(2)}) copy-start(f32[64,128]{1,0:T(8,128)} %get-tuple-element.18.one_ref) | copy-start | bytes 98308

commit v3 on v2

--- a/solution.py
+++ b/solution.py
@@ -44,9 +44,11 @@
 
 def kernel(
     nal, ncr, nsu, factor,
-    state_ref, storm_ref, wet_ref, dune_ref, cid_ref,
-    w1_ref, b1_ref, w2_ref, b2_ref, wo_ref, bo_ref, cot_ref,
-    gstate_ref, full_one, full_two,
+    state_hbm, cid_hbm, w1_hbm, b1_hbm, w2_hbm, b2_hbm, wo_hbm, bo_hbm,
+    storm_hbm, wet_hbm, dune_hbm, cot_hbm,
+    gstate_hbm, one_hbm, two_hbm,
+    state_ref, cid_ref, w1_ref, b1_ref, w2_ref, b2_ref, wo_ref, bo_ref,
+    storm_ref, wet_ref, dune_ref, cot_ref, gstate_ref, load_sem, store_sem,
     snd_row, snd_col, rcv_row, rcv_col, send_sem, recv_sem,
     feat_ref, dfeat_ref, z_ref, dz_ref,
     b1b_ref, b2b_ref, wsel_ref,
@@ -72,18 +74,36 @@
         dev(al - 1, cs), dev(al + 1, cs), dev(al, cs - 1), dev(al, cs + 1),
     )
 
+    loads = [
+        pltpu.make_async_copy(src, dst, load_sem.at[i])
+        for i, (src, dst) in enumerate((
+            (state_hbm, state_ref), (cid_hbm, cid_ref), (w1_hbm, w1_ref), (b1_hbm, b1_ref),
+            (w2_hbm, w2_ref), (b2_hbm, b2_ref), (wo_hbm, wo_ref), (bo_hbm, bo_ref),
+            (storm_hbm, storm_ref), (wet_hbm, wet_ref), (dune_hbm, dune_ref), (cot_hbm, cot_ref),
+        ))
+    ]
+    loads[0].start()
     rcv_row[...] = jnp.zeros_like(rcv_row)
     rcv_col[...] = jnp.zeros_like(rcv_col)
 
     barrier = pltpu.get_barrier_semaphore()
-    for j in range(1, ncs):
-        pl.semaphore_signal(
-            barrier, inc=1, device_id=dev(al, lax.rem(cs + j, ncs)), device_id_type=MESH
-        )
-    for j in range(1, nal):
-        pl.semaphore_signal(
-            barrier, inc=1, device_id=dev(lax.rem(al + j, nal), cs), device_id_type=MESH
-        )
+    near_only = nal <= 4 and ncs <= 4
+    if near_only:
+        for d in range(4):
+            @pl.when(has_dst[d])
+            def _():
+                pl.semaphore_signal(barrier, inc=1, device_id=dst_dev[d], device_id_type=MESH)
+    else:
+        for j in range(1, ncs):
+            pl.semaphore_signal(
+                barrier, inc=1, device_id=dev(al, lax.rem(cs + j, ncs)), device_id_type=MESH
+            )
+        for j in range(1, nal):
+            pl.semaphore_signal(
+                barrier, inc=1, device_id=dev(lax.rem(al + j, nal), cs), device_id_type=MESH
+            )
+    for load in loads[1:]:
+        load.start()
 
     row = lax.broadcasted_iota(jnp.int32, (8, 128), 0)
     lane = lax.broadcasted_iota(jnp.int32, (8, 128), 1)
@@ -140,10 +160,18 @@
         halo = rcv_col[k, 1]
         return jnp.where(lane == 0, pltpu.roll(halo, 128 - f, 1) if f else halo, pltpu.roll(x, 1, 1))
 
+    loads[0].wait()
     V0 = [state_ref[f] for f in range(12)]
     fill(0, V0, V0, V0, V0)
-    pl.semaphore_wait(barrier, ncs - 1 + nal - 1)
+    if near_only:
+        beside = (al + nal - 1) // nal + (2 * nal - 2 - al) // nal
+        beside = beside + (cs + ncs - 1) // ncs + (2 * ncs - 2 - cs) // ncs
+        pl.semaphore_wait(barrier, beside)
+    else:
+        pl.semaphore_wait(barrier, ncs - 1 + nal - 1)
     launch(0)
+    for load in loads[1:]:
+        load.wait()
 
     w1 = w1_ref[...]
     w1t = jnp.transpose(jnp.concatenate([w1, jnp.zeros((96, 128), f32)], axis=0))[:, :32]
@@ -169,7 +197,7 @@
         )
     bsel = jnp.zeros((8, 128), f32)
     for k in range(8):
-        bsel = jnp.where(cid == k, bo_ref[k], bsel)
+        bsel = jnp.where(cid == k, bo_ref[0:1, k:k + 1], bsel)
     for f in range(12):
         feat_ref[(20 + f) * 8:(21 + f) * 8, :] = storm_ref[f]
     wets = [wet_ref[t].astype(f32) for t in range(2)]
@@ -449,15 +477,24 @@
     last = gather(c0, to0, 3)
     for f in range(12):
         gstate_ref[f] = last[f]
+    stores = [
+        pltpu.make_async_copy(src, dst, store_sem.at[i])
+        for i, (src, dst) in enumerate(
+            ((gstate_ref, gstate_hbm), (dst_one, one_hbm), (dst_two, two_hbm))
+        )
+    ]
+    stores[0].start()
     sum_one.third()
     sum_two.fourth()
-    full_two[...] = dst_two[...]
+    stores[2].start()
     sum_one.fourth()
-    full_one[...] = dst_one[...]
+    stores[1].start()
     for k in range(4):
         finish_sends(k)
     sum_two.sends()
     sum_one.sends()
+    for store in stores:
+        store.wait()
 
 
 def unpack(state_ref, one_ref, two_ref, gs_ref, gw1_ref, gb1_ref, gw2_ref, gb2_ref, gwo_ref, gbo_ref):
@@ -481,7 +518,11 @@
         rows, cols = state.shape[1], state.shape[2]
         factor = 1.0 / math.sqrt(rows * nal * cols * ncs)
         vmem = pl.BlockSpec(memory_space=pltpu.VMEM)
-        smem = pl.BlockSpec(memory_space=pltpu.SMEM)
+        hbm = pl.BlockSpec(memory_space=pl.ANY)
+        operands = (
+            state, cid, w1, b1.reshape(1, 128), w2, b2.reshape(1, 128), wo.T, bo.reshape(1, 8),
+            storm, wet, dune, cot,
+        )
         dma = pltpu.SemaphoreType.DMA
         big = lambda n, kind: pltpu.VMEM((2, n, 1024), kind)
         summed = lambda n: [
@@ -498,9 +539,11 @@
                 jax.ShapeDtypeStruct((ncs * rows_one, 128), f32),
                 jax.ShapeDtypeStruct((ncs * rows_two, 128), f32),
             ),
-            in_specs=[vmem] * 10 + [smem, vmem],
-            out_specs=(vmem,) * 3,
+            in_specs=[hbm] * 12,
+            out_specs=(hbm,) * 3,
             scratch_shapes=[
+                *[pltpu.VMEM(x.shape, x.dtype) for x in operands],
+                pltpu.VMEM((12, 8, 128), f32), dma((12,)), dma((3,)),
                 pltpu.VMEM((4, 2, 16, 128), f32),
                 pltpu.VMEM((4, 2, 8, 128), f32),
                 pltpu.VMEM((4, 2, 16, 128), f32),
@@ -520,7 +563,7 @@
                 dma((2, ncs)), dma((2, ncs)), dma((2, nal)), dma((2, nal)), dma((2, ncs)), dma((2, ncs)),
             ],
             compiler_params=pltpu.CompilerParams(collective_id=0, has_side_effects=True),
-        )(state, storm, wet, dune, cid, w1, b1.reshape(1, 128), w2, b2.reshape(1, 128), wo.T, bo, cot)
+        )(*operands)
         gs, gw1, gb1, gw2, gb2, gwo, gbo = pl.pallas_call(
             unpack,
             out_shape=(
@@ -534,7 +577,6 @@
             ),
             in_specs=[vmem] * 3,
             out_specs=(vmem,) * 7,
-            compiler_params=pltpu.CompilerParams(vmem_limit_bytes=4 << 20),
         )(*out)
         return gs, gw1, gb1.reshape(128), gw2, gb2.reshape(128), gwo.T, gbo.reshape(8)
 

time: 34 us -> 30.3 us (0.89)
  local copies, waits for them, and re-layouts: 2.44 us -> 0 us
  Pallas kernels: 30.5 us -> 29.4 us
    unnamed x6 -> x0, local copies, waits for them, and re-layouts: 2.44 us -> none
    pallas_call x1, Pallas kernels: 29.9 us -> 27.8 us  [per_device(): pl.pallas_call(functools.partial(kernel, nal, ncr, nsu, factor), out_shap...]
    pallas_call x1, Pallas kernels: 0.66 us -> 1.6 us  [per_device(): pl.pallas_call(unpack, out_shape=(jax.ShapeDtypeStruct((12, 8, 128), f32)...]
where the time goes in v3:
time: 30.3 us; the launch traced here: 30.1 us
  Pallas kernels  29.4 us (97%)
  between operations  0.65 us (2%)
    pallas_call x1, Pallas kernels, per_device(): pl.pallas_call(functools.partial(kernel, nal, ncr, nsu, factor), out_shap...  27.8 us
    pallas_call x1, Pallas kernels, per_device(): pl.pallas_call(unpack, out_shape=(jax.ShapeDtypeStruct((12, 8, 128), f32)...  1.6 us

profile of v3, /device:TPU:0, one launch (start us, length us, event | category | flops | bytes accessed | tf_op | source)
XLA Modules:
  0.0 30.1 jit_solution(1396095144789233304)
XLA Ops:
  0.6 27.8 %shard_map.171 = (f32[12,8,128]{2,1,0:T(8,128)}, f32[64,128]{1,0:T(8,128)}, f32[160,128]{1,0:T(8,128)}) custom-call(f32[12,8,128]{2,1,0:T(8,128)} %state_hbm.1, s32[8,128]{1,0:T(8,128)} %cid_hbm.1, f32[32,128]{1,0:T(8,128)} %w1_hbm.1, f32[1,128]{1,0:T(1,128)} %bitcast.9, f32[128,128]{1,0:T(8,128)} %w2_hbm.1, f32[1,128]{1,0:T(1,128)} %bitcast.10, ...), custom_call_target="tpu_custom_call" | custom-call | tf_op jit(solution)/shard_map/pallas_call | solution.py:535
  28.5 1.6 %shard_map.172 = (f32[12,8,128]{2,1,0:T(8,128)}, f32[32,128]{1,0:T(8,128)}, f32[1,128]{1,0:T(1,128)}, f32[128,128]{1,0:T(8,128)}, f32[1,128]{1,0:T(1,128)}, /*index=5*/f32[8,128]{1,0:T(8,128)}, f32[1,8]{1,0:T(1,128)}) custom-call(f32[12,8,128]{2,1,0:T(8,128)} %get-tuple-element.17.state_ref, f32[64,128]{1,0:T(8,128)} %get-tuple-element.18.one_ref, ...), custom_call_target="tpu_custom_call" | custom-call | tf_op jit(solution)/shard_map/pallas_call | solution.py:567

commit v4 on v3

--- a/solution.py
+++ b/solution.py
@@ -226,7 +226,7 @@
             v = mm(w1t_cat, jnp.concatenate([Fh, Fh, Fl], axis=0))
             bias = b1b_ref[...]
             v = v + jnp.concatenate([bias, bias], axis=1)
-            sig = 1.0 / (1.0 + jnp.exp(-v))
+            sig = 0.5 + 0.5 * jnp.tanh(0.5 * v)
             h = v * sig
             act1_ref[t, :, at] = sig + h * (1.0 - sig)
             Hh, Hl = split(h)
@@ -235,7 +235,7 @@
             v = mm(w2t_hh, jnp.concatenate([Hh, Hl], axis=0)) + mm(w2tl, Hh)
             bias = b2b_ref[...]
             v = v + jnp.concatenate([bias, bias], axis=1)
-            sig = 1.0 / (1.0 + jnp.exp(-v))
+            sig = 0.5 + 0.5 * jnp.tanh(0.5 * v)
             h = v * sig
             wsel = wsel_ref[:, at]
             q2_ref[t, :, at] = wsel * (sig + h * (1.0 - sig))
@@ -467,12 +467,11 @@
     adjoint_one(0)
     weights_one(0, False)
     sum_one.first()
-    sum_two.second()
     c0, to0 = adjoint_cells(0, G0, near0, V0, lam1)
     fill(3, *to0)
     launch(3)
+    sum_two.second()
     sum_one.second()
-    sum_two.third()
     finish(3)
     last = gather(c0, to0, 3)
     for f in range(12):
@@ -484,6 +483,7 @@
         )
     ]
     stores[0].start()
+    sum_two.third()
     sum_one.third()
     sum_two.fourth()
     stores[2].start()

time: 30.3 us -> 29.9 us (0.987)
    pallas_call x1, Pallas kernels: 27.8 us -> 27.5 us  [per_device(): pl.pallas_call(functools.partial(kernel, nal, ncr, nsu, factor), out_shap...]
where the time goes in v4:
time: 29.9 us; the launch traced here: 29.7 us
  Pallas kernels  29.1 us (97%)
  between operations  0.65 us (2%)
    pallas_call x1, Pallas kernels, per_device(): pl.pallas_call(functools.partial(kernel, nal, ncr, nsu, factor), out_shap...  27.5 us
    pallas_call x1, Pallas kernels, per_device(): pl.pallas_call(unpack, out_shape=(jax.ShapeDtypeStruct((12, 8, 128), f32)...  1.6 us

profile of v4, /device:TPU:0, one launch (start us, length us, event | category | flops | bytes accessed | tf_op | source)
XLA Modules:
  0.0 29.7 jit_solution(13852651280419112400)
XLA Ops:
  0.6 27.5 %shard_map.171 = (f32[12,8,128]{2,1,0:T(8,128)}, f32[64,128]{1,0:T(8,128)}, f32[160,128]{1,0:T(8,128)}) custom-call(f32[12,8,128]{2,1,0:T(8,128)} %state_hbm.1, s32[8,128]{1,0:T(8,128)} %cid_hbm.1, f32[32,128]{1,0:T(8,128)} %w1_hbm.1, f32[1,128]{1,0:T(1,128)} %bitcast.9, f32[128,128]{1,0:T(8,128)} %w2_hbm.1, f32[1,128]{1,0:T(1,128)} %bitcast.10, ...), custom_call_target="tpu_custom_call" | custom-call | tf_op jit(solution)/shard_map/pallas_call | solution.py:535
  28.1 1.6 %shard_map.172 = (f32[12,8,128]{2,1,0:T(8,128)}, f32[32,128]{1,0:T(8,128)}, f32[1,128]{1,0:T(1,128)}, f32[128,128]{1,0:T(8,128)}, f32[1,128]{1,0:T(1,128)}, /*index=5*/f32[8,128]{1,0:T(8,128)}, f32[1,8]{1,0:T(1,128)}) custom-call(f32[12,8,128]{2,1,0:T(8,128)} %get-tuple-element.17.state_ref, f32[64,128]{1,0:T(8,128)} %get-tuple-element.18.one_ref, ...), custom_call_target="tpu_custom_call" | custom-call | tf_op jit(solution)/shard_map/pallas_call | solution.py:567
